TPU v7x, 32 devices: a whole 2x2x4 slice. The times are simulated.
32 devices in a mesh: section: 4 (over y, x), dp: 8 (over z, core).
Axes of the slice: x: 2, y: 2, z: 4, core: 2. Of those that a mesh axis runs over, the one named last changes fastest.
Arguments:
- tokens: bfloat16 [2, 4, 448, 2048], P(None, None, 'dp'), may hold values from -6 to 6
- targets: bfloat16 [2, 4, 448, 2048], P(None, None, 'dp'), may hold values from -6 to 6
- weights: bfloat16 [4, 2, 2, 96, 128, 128], P('section'), as said below
- pattern: int32 [4, 2, 2, 96, 2], P('section'), may hold values from 0 to 63, as said below
- master: float32 [4, 2, 96, 128, 128], P('section', None, None, 'dp'), may hold values from -0.6 to 0.6
- moment: float32 [4, 2, 96, 128, 128], P('section', None, None, 'dp'), as said below
- variance: float32 [4, 2, 96, 128, 128], P('section', None, None, 'dp'), as said below
Outputs:
- adam_step: float32 [4, 2, 96, 128, 128], P('section', None, None, 'dp')
- new_master: float32 [4, 2, 96, 128, 128], P('section', None, None, 'dp')
Inputs may be any that keep to these rules, and one draw needn't show every extreme that they name: Within one layer and projection the 96 blocks are distinct and sorted; every block column of the up projection and every block row of the down projection holds one or more blocks. pattern[s,1] equals pattern[3 - s, 0]. Up blocks have rows below 16 and columns below 64, down blocks the reverse. weights[s,1] equals weights[3 - s, 0]; entries are scaled by the inverse root of the mean number of inputs per output. `moment`: of the order of the gradient. `variance`: Positive, of the order of the squared gradient.
All inputs are finite; a program needn't handle non-finite values.
Results may differ from a plain program's by a relative error of at most 0.022.
Values may be sent and summed in bfloat16 or wider, within the bound.
No kernel may reach another device: no remote copies, remote signals or barrier semaphores. Data moves between devices by JAX's collectives and lax.ppermute only.
A program may use at most 192 MiB of HBM per device.

v0:
```python
import jax
import jax.numpy as jnp
from jax import lax
from jax.experimental import pallas as pl
from jax.experimental.pallas import tpu as pltpu
from jax.sharding import PartitionSpec as P


BS = 128
FF_BLOCKS = 8192 // BS
norm_eps = 1e-06
gelu_coef = 0.7978845608028654
gelu_cubic = gelu_coef * 0.044715
beta_first = 0.9
beta_second = 0.95
adam_eps = 1e-08
learn_rate = 0.001
decay_rate = 0.1
update_count = 10
ROW_TILE = 16
EXTRA_BATCH = 4
CHAIN_VMEM = 24 * 1024 * 1024
ENTER_VMEM = 32 * 1024 * 1024
OWN_VMEM = 40 * 1024 * 1024
COST = 4_000_000_000
LOCAL = None
ENTER_COST = 1
LOW_LAYER, HIGH_LAYER, OWN_LAYER, HIGH, GROUP = range(5)
UP_WIDE, DOWN_WIDE, DOWN_NARROW, UP_NARROW = range(4)
FIELDS = 9
FIRST, FIRST_TAKE, SECOND, SECOND_TAKE, PUT, EXTRA, EXTRA_TAKE, EXTRA_PUT, COUNT = range(FIELDS)


def block_lists(pattern, width):
    total = pattern.shape[2]
    up_row, up_col = pattern[:, 0, :, 0], pattern[:, 0, :, 1]
    down_row, down_col = pattern[:, 1, :, 0], pattern[:, 1, :, 1]
    key = jnp.stack([up_col, down_row, down_col, up_row], 1)
    take = jnp.stack([up_row, down_col, down_row, up_col], 1)
    order = jnp.arange(total, dtype=jnp.int32)
    before = order[None, :] < order[:, None]

    def count(mask):
        return jnp.sum(mask.astype(jnp.int32), axis=-1)

    same = key[..., None, :] == key[..., :, None]
    rank = count(same & before)
    even = rank % 2 == 0
    wide = (jnp.arange(4) < 2)[None, :, None]
    extra = rank >= 2
    extra_place = count(extra[..., None, :] & before)
    pair = count((key[..., None, :] < key[..., :, None]) & even[..., None, :]) + rank // 2
    place_first = jnp.where(wide, jnp.where(rank == 0, key, -1), jnp.where(even, pair, -1))
    place_second = jnp.where(wide, jnp.where(rank == 1, key, -1), jnp.where(even, -1, pair))
    place_extra = jnp.where(wide & extra, extra_place, -1)
    number = jnp.broadcast_to(order, key.shape)
    places = jnp.stack(
        [place_first] * 2 + [place_second] * 2 + [place_first] + [place_extra] * 3, 2
    )
    absent = jnp.where(wide, width // BS, FF_BLOCKS)
    lowered = take - absent
    values = jnp.stack([number, lowered, number, lowered, key, number, lowered, key], 2)
    hit = places[..., None, :] == order[:, None]
    fields = jnp.sum(jnp.where(hit, values[..., None, :], 0), axis=-1)
    slot = jnp.arange(8)
    taken = (slot == FIRST_TAKE) | (slot == SECOND_TAKE) | (slot == EXTRA_TAKE)
    fields = fields + jnp.where(taken[:, None], absent[..., None], 0)
    counts = jnp.where(wide[..., 0], count(extra), count(even))
    counts = jnp.broadcast_to(counts[..., None, None], key.shape[:2] + (1, total))
    lists = jnp.concatenate([fields, counts], axis=2).astype(jnp.int32)
    return jnp.concatenate([lists.reshape(-1), pattern[0].reshape(-1)])


class Lists:
    def __init__(self, ref, copy, total):
        self.ref, self.total = ref, total
        self.base = copy * (4 * FIELDS * total)
        self.cells = 2 * 4 * FIELDS * total

    def __call__(self, kind, field, index):
        return self.ref[self.base + ((kind * FIELDS + field) * self.total) + index]


def hidden_of(preact):
    inner = preact * (gelu_coef + gelu_cubic * (preact * preact))
    half = 0.5 * preact
    return half + half * jnp.tanh(inner)


def both_of(preact):
    cubic = gelu_cubic * (preact * preact)
    tangent = jnp.tanh(preact * (gelu_coef + cubic))
    bend = preact * (gelu_coef + 3.0 * cubic)
    half = 0.5 + 0.5 * tangent
    return (preact * half, half * (1.0 + bend * (1.0 - tangent)))


def dot_plain(left, right):
    return jnp.dot(left, right, preferred_element_type=jnp.float32)


def dot_right_t(left, right):
    return lax.dot_general(left, right, (((1,), (1,)), ((), ())), preferred_element_type=jnp.float32)


def each(count, body, unroll=1):
    def one(i, carry):
        body(i)
        return carry

    lax.fori_loop(0, count, one, 0, unroll=unroll)


def fill_normed(x_ref, normed, base):
    rows, width = x_ref.shape

    def tile(i):
        at = pl.multiple_of(i * ROW_TILE, ROW_TILE)
        wide = x_ref[pl.ds(at, ROW_TILE), :].astype(jnp.float32)
        factor = lax.rsqrt(jnp.mean(wide * wide, axis=-1, keepdims=True) + norm_eps)
        value = (wide * factor).astype(jnp.bfloat16)
        for b in range(width // BS):
            normed[b, pl.ds(base + at, ROW_TILE), :] = value[:, b * BS : (b + 1) * BS]

    each(rows // ROW_TILE, tile, 7)


def fill_split(x_ref, split, base):
    rows, width = x_ref.shape
    for b in range(width // BS):
        split[b, pl.ds(base, rows), :] = x_ref[:, b * BS : (b + 1) * BS]


def pair_product(source, blocks, lists, kind, p, transposed):
    left = jnp.concatenate(
        [source[lists(kind, FIRST_TAKE, p)], source[lists(kind, SECOND_TAKE, p)]], axis=1
    )
    one, two = blocks[lists(kind, FIRST, p)], blocks[lists(kind, SECOND, p)]
    if transposed:
        return dot_right_t(left, jnp.concatenate([one, two], axis=1))
    return dot_plain(left, jnp.concatenate([one, two], axis=0))


def wide_pass(source, blocks, lists, kind, sums, finish, transposed, batch=16, ahead=None):
    def main(i):
        if ahead is not None:
            ahead(i)
        for j in range(batch):
            c = i * batch + j
            value = pair_product(source, blocks, lists, kind, c, transposed)
            sums[c] = value
            finish(c, value)

    each(sums.shape[0] // batch, main)
    dot = dot_right_t if transposed else dot_plain

    def more(e):
        c = lists(kind, EXTRA_PUT, e)
        left = source[lists(kind, EXTRA_TAKE, e)]
        value = sums[c] + dot(left, blocks[lists(kind, EXTRA, e)])
        sums[c] = value
        finish(c, value)

    def batch(i):
        for j in range(EXTRA_BATCH):
            more(i * EXTRA_BATCH + j)

    each((lists(kind, COUNT, 0) + EXTRA_BATCH - 1) // EXTRA_BATCH, batch)


def narrow_pass(source, blocks, lists, kind, sums, transposed):
    sums[...] = jnp.zeros(sums.shape, sums.dtype)

    def one(p):
        sums[lists(kind, PUT, p)] += pair_product(source, blocks, lists, kind, p, transposed)

    each((lists.total + sums.shape[0]) // 2, one, 14)


def forward_rows(x_ref, out_ref, layer, scratch, slopes=None, before=lambda part: None, done=lambda: None):
    normed, sums, hidden, narrow = scratch
    _, width = x_ref.shape
    fill_normed(x_ref, normed, 0)

    def finish(c, value):
        if slopes is None:
            hidden[c] = hidden_of(value).astype(jnp.bfloat16)
        else:
            value, slope = both_of(value)
            hidden[c] = value.astype(jnp.bfloat16)
            slopes[c] = slope.astype(slopes.dtype)

    before(0)
    wide_pass(normed, layer.up, layer.lists, UP_WIDE, sums, finish, False)
    before(1)
    done()
    narrow_pass(hidden, layer.down, layer.lists, DOWN_NARROW, narrow, False)
    for b in range(width // BS):
        cols = slice(b * BS, (b + 1) * BS)
        out_ref[:, cols] = (x_ref[:, cols].astype(jnp.float32) + narrow[b]).astype(jnp.bfloat16)


def backward_rows(x_ref, cot_ref, out_ref, layer, scratch, slopes, ready=lambda: None):
    normed, sums, hidden, narrow = scratch
    rows, width = x_ref.shape
    fill_split(cot_ref, normed, 0)
    ready()

    def finish(c, value):
        hidden[c] = (value * slopes[c].astype(jnp.float32)).astype(jnp.bfloat16)

    wide_pass(normed, layer.down, layer.lists, DOWN_WIDE, sums, finish, True)
    narrow_pass(hidden, layer.up, layer.lists, UP_NARROW, narrow, True)

    def tile(i):
        at = pl.multiple_of(i * ROW_TILE, ROW_TILE)
        wide = x_ref[pl.ds(at, ROW_TILE), :].astype(jnp.float32)
        factor = lax.rsqrt(jnp.mean(wide * wide, axis=-1, keepdims=True) + norm_eps)
        grad = jnp.concatenate(
            [narrow[b, pl.ds(at, ROW_TILE), :] for b in range(width // BS)], axis=-1
        )
        coupling = jnp.mean(wide * grad, axis=-1, keepdims=True)
        upstream = cot_ref[pl.ds(at, ROW_TILE), :].astype(jnp.float32)
        value = upstream + factor * grad - wide * (factor * factor * factor * coupling)
        out_ref[pl.ds(at, ROW_TILE), :] = value.astype(jnp.bfloat16)

    each(rows // ROW_TILE, tile)


def own_cell(layer, part, k):
    lists = layer.lists
    at = lists.cells + 2 * (part * lists.total + k)
    return lists.ref[at], lists.ref[at + 1]


class Layer:
    def __init__(self, info, lists_ref, weights_ref, which, local=None):
        copy = info[which]
        self.lists = Lists(lists_ref, copy, lists_ref.shape[0] // (2 * 4 * FIELDS + 4))
        if weights_ref is not None:
            local = weights_ref.at[copy]
        if local is not None:
            self.up, self.down = local.at[0], local.at[1]


def stage(kernel, local_in, remote_in, outs, scratch, operands, cost, vmem=CHAIN_VMEM):
    info, lists, weights = operands
    held = [] if weights is None else [pltpu.with_memory_space_constraint(weights, pltpu.VMEM)]
    any_spec = pl.BlockSpec(memory_space=pltpu.HBM)
    smem_spec = pl.BlockSpec(memory_space=pltpu.SMEM)
    vmem_spec = pl.BlockSpec(memory_space=pltpu.VMEM)
    in_total = len(local_in) + len(remote_in)
    local_in = [pltpu.with_memory_space_constraint(array, pltpu.VMEM) for array in local_in]

    def body(info_ref, lists_ref, *rest):
        weights_ref, rest = (None, rest) if weights is None else (rest[0], rest[1:])
        ins, own = rest[:in_total], rest[in_total + len(outs) :]
        results = rest[in_total : in_total + len(outs)]

        def layer(which, weights_ref=weights_ref, local=None):
            return Layer(info_ref, lists_ref, weights_ref, which, local)

        kernel(layer, info_ref, ins, results, own)

    return pl.pallas_call(
        body,
        in_specs=[smem_spec, smem_spec]
        + [vmem_spec] * (len(held) + len(local_in))
        + [any_spec] * len(remote_in),
        out_specs=[any_spec if space is pltpu.HBM else vmem_spec for space, _ in outs],
        out_shape=[
            shape if space is LOCAL else space(shape.shape, shape.dtype) for space, shape in outs
        ],
        scratch_shapes=scratch,
        cost_estimate=pl.CostEstimate(flops=cost, transcendentals=0, bytes_accessed=0),
        compiler_params=pltpu.CompilerParams(vmem_limit_bytes=vmem),
    )(info, lists, *held, *local_in, *remote_in)


def layer_scratch(rows, width):
    return [
        pltpu.VMEM((width // BS + 1, rows, BS), jnp.bfloat16),
        pltpu.VMEM((FF_BLOCKS, rows, BS), jnp.float32),
        pltpu.VMEM((FF_BLOCKS + 1, rows, BS), jnp.bfloat16),
        pltpu.VMEM((width // BS, rows, BS), jnp.float32),
    ]


def slope_scratch(rows):
    return [pltpu.VMEM((FF_BLOCKS, rows, BS), jnp.float32)]


def shape_of(shape, dtype=jnp.bfloat16):
    return jax.ShapeDtypeStruct(shape, dtype)


def clear_spare(*refs):
    for ref in refs:
        ref[ref.shape[0] - 1] = jnp.zeros(ref.shape[1:], ref.dtype)


def forward_call(x, whichs, operands):
    rows, width = x.shape
    steps = len(whichs)
    slope_shape = (steps, FF_BLOCKS, rows, BS)

    def kernel(layer, info, ins, results, scratch):
        *layer_refs, slopes, sem = scratch
        clear_spare(layer_refs[0], layer_refs[2])
        moves = [
            pltpu.make_async_copy(slopes.at[i], results[-1].at[i], sem.at[i]) for i in range(steps)
        ]
        source = ins[0]
        for i, which in enumerate(whichs):
            forward_rows(
                source, results[i], layer(which), layer_refs, slopes.at[i], done=moves[i].start
            )
            source = results[i]
        for move in moves:
            move.wait()

    outs = [(LOCAL, shape_of(x.shape))] * steps + [(pltpu.HBM, shape_of(slope_shape))]
    scratch = [pltpu.VMEM(slope_shape, jnp.bfloat16), pltpu.SemaphoreType.DMA((steps,))]
    return stage(
        kernel, [x], [], outs, layer_scratch(rows, width) + scratch, operands, COST * steps
    )


def enter_call(tokens, h, rows, unloaded, operands):
    width = tokens.shape[-1]

    def kernel(layer, info, ins, results, scratch):
        *layer_refs, x_ref, local, sem, weight_sem = scratch
        load = pltpu.make_async_copy(ins[0].at[info[HIGH], pl.ds(h * rows, rows)], x_ref, sem)
        load.start()
        low = info[LOW_LAYER]
        moves = [
            pltpu.make_async_copy(ins[1].at[low, part], local.at[part], weight_sem.at[part])
            for part in range(2)
        ]

        def before(part):
            moves[part].wait()
            if part == 0:
                moves[1].start()

        moves[0].start()
        clear_spare(layer_refs[0], layer_refs[2])
        load.wait()
        forward_rows(x_ref, results[0], layer(LOW_LAYER, None, local), layer_refs, before=before)

    outs = [(LOCAL, shape_of((rows, width)))]
    scratch = layer_scratch(rows, width) + [
        pltpu.VMEM((rows, width), jnp.bfloat16),
        pltpu.VMEM(unloaded.shape[1:], unloaded.dtype),
        pltpu.SemaphoreType.DMA,
        pltpu.SemaphoreType.DMA((2,)),
    ]
    return stage(kernel, [], [tokens, unloaded], outs, scratch, operands, COST * ENTER_COST, CHAIN_VMEM)


def turn_call(x, targets, h, operands, entries=None):
    rows, width = x.shape
    local = [x] + ([] if entries is None else [e for pair in entries for e in pair])

    def kernel(layer, info, ins, results, scratch):
        *layer_refs, slopes, aim, sem = scratch
        x_ref, target_ref = ins[0], ins[-1]
        residue, out = results[:2]
        load = pltpu.make_async_copy(target_ref.at[info[HIGH], pl.ds(h * rows, rows)], aim, sem)
        load.start()
        clear_spare(layer_refs[0], layer_refs[2])
        own = layer(HIGH_LAYER)
        forward_rows(x_ref, residue, own, layer_refs, slopes)
        load.wait()
        for b in range(width // BS):
            cols = slice(b * BS, (b + 1) * BS)
            difference = residue[:, cols].astype(jnp.float32) - aim[:, cols].astype(jnp.float32)
            residue[:, cols] = difference.astype(jnp.bfloat16)
        backward_rows(x_ref, residue, out, own, layer_refs, slopes)
        if entries is not None:
            high, group = info[HIGH] == 1, info[GROUP]
            conditions = [~high & (group == 0), ~high & (group != 0), high]
            for i in range(2):
                sources = [ins[1 + 2 * j + i] for j in range(3)]
                pick_rows(results[2].at[pl.ds(i * rows, rows)], list(zip(conditions, sources)))

    outs = [(LOCAL, shape_of(x.shape))] * 2
    if entries is not None:
        outs.append((LOCAL, shape_of((2 * rows, width))))
    return stage(
        kernel, local, [targets], outs,
        layer_scratch(rows, width) + slope_scratch(rows)
        + [pltpu.VMEM((rows, width), jnp.bfloat16), pltpu.SemaphoreType.DMA],
        operands, 3 * COST
    )


def pick_rows(target, options):
    for condition, source in options:

        @pl.when(condition)
        def take(source=source):
            target[...] = source[...]


def backward_call(xs, saved, cot, whichs, operands, turned=None, last=None):
    rows, width = cot.shape
    steps = len(whichs)
    local = list(xs) + [cot] + ([] if turned is None else [turned])

    def kernel(layer, info, ins, results, scratch):
        *layer_refs, slopes, sem = scratch
        moves = [
            pltpu.make_async_copy(ins[len(local) + i].at[saved[i][1]], slopes.at[i], sem.at[i])
            for i in range(steps)
        ]
        for move in moves:
            move.start()
        clear_spare(layer_refs[0], layer_refs[2])
        upstream = ins[steps]
        for i, which in enumerate(whichs):
            backward_rows(
                ins[i], upstream, results[i], layer(which), layer_refs, slopes.at[i], moves[i].wait
            )
            upstream = results[i]
        if turned is not None:
            high, group = info[HIGH] == 1, info[GROUP]
            pick_rows(
                results[steps],
                [
                    (high, results[0]),
                    (~high & (group == last), ins[steps]),
                    (~high & (group != last), ins[steps + 1]),
                ],
            )

    scratch = [
        pltpu.VMEM((steps, FF_BLOCKS, rows, BS), jnp.bfloat16),
        pltpu.SemaphoreType.DMA((steps,)),
    ]
    outs = [(LOCAL, shape_of(cot.shape))] * (steps + (turned is not None))
    return stage(
        kernel, local, [array for array, _ in saved], outs, layer_scratch(rows, width) + scratch,
        operands, 2 * COST * steps
    )


def fetch_pieces(info, choices, refs, local, sem):
    first = (info[HIGH] == 0) & (info[GROUP] == 0)
    moves = []
    for piece, options in enumerate(choices):
        for kind, wanted, number, index in options:
            source = refs[number] if index is None else refs[number].at[index]
            move = pltpu.make_async_copy(source, local.at[piece], sem.at[piece])
            if kind == "first":
                condition = first
            elif kind == "own":
                condition = (info[HIGH] == wanted[0]) & (info[GROUP] == wanted[1]) & ~first
            else:
                condition = ~first

            @pl.when(condition)
            def go(move=move):
                move.start()

        moves.append(move)
    return moves


def ups_call(refs, choices, after, rows, width, unloaded, operands):
    pieces = len(choices)
    all_rows = rows * pieces
    part_rows = all_rows // 2

    def kernel(layer, info, ins, results, scratch):
        x_refs, sums, blocks_here, slopes, normed, sem, block_sem, out_sem = scratch
        hidden, slopes_out, normed_out = results
        load = pltpu.make_async_copy(ins[-1].at[0, 0], blocks_here, block_sem.at[0])
        load.start()
        moves = fetch_pieces(info, choices, ins, x_refs, sem)
        own = layer(OWN_LAYER)
        clear_spare(normed)
        for move in moves:
            move.wait()

        def normalise(piece):
            fill_normed(x_refs.at[piece], normed, piece * rows)

        each(pieces, normalise)
        keep = pltpu.make_async_copy(normed, normed_out, block_sem.at[1])
        keep.start()
        load.wait()

        def put(part):
            span = pl.ds(pl.multiple_of(part * part_rows, part_rows), part_rows)
            return pltpu.make_async_copy(slopes.at[part], slopes_out.at[:, span], out_sem.at[part])

        def one(part):
            span = pl.ds(pl.multiple_of(part * part_rows, part_rows), part_rows)

            def finish(c, value):
                value, slope = both_of(value)
                hidden[c, span, :] = value.astype(jnp.bfloat16)
                slopes[part, c] = slope.astype(jnp.bfloat16)

            wide_pass(
                normed.at[:, span], blocks_here, own.lists, UP_WIDE, sums, finish, False, 8
            )
            put(part).start()

        each(2, one)
        keep.wait()
        for part in range(2):
            put(part).wait()

    return stage(
        kernel, [], refs + [after, unloaded],
        [
            (pltpu.VMEM, shape_of((FF_BLOCKS, all_rows, BS))),
            (pltpu.HBM, shape_of((FF_BLOCKS, all_rows, BS))),
            (pltpu.HBM, shape_of((width // BS + 1, all_rows, BS))),
        ],
        [
            pltpu.VMEM((pieces, rows, width), jnp.bfloat16),
            pltpu.VMEM((FF_BLOCKS, part_rows, BS), jnp.float32),
            pltpu.VMEM(unloaded.shape[2:], unloaded.dtype),
            pltpu.VMEM((2, FF_BLOCKS, part_rows, BS), jnp.bfloat16),
            pltpu.VMEM((width // BS + 1, all_rows, BS), jnp.bfloat16),
            pltpu.SemaphoreType.DMA((pieces,)),
            pltpu.SemaphoreType.DMA((2,)),
            pltpu.SemaphoreType.DMA((2,)),
        ],
        operands, 4 * COST, ENTER_VMEM
    )


def spread(out, k, value, shares):
    share_rows = BS // shares
    for share in range(shares):
        out[share, k] = value[share * share_rows : (share + 1) * share_rows]


def down_grads_call(refs, choices, hidden, rows, width, shares, total, operands):
    pieces = len(choices)
    all_rows = rows * pieces

    def kernel(layer, info, ins, results, scratch):
        cot_refs, split, turned, sem, out_sem = scratch
        out, split_out = results
        hidden_ref, refs = ins[0], ins[1:]
        own = layer(OWN_LAYER)
        moves = fetch_pieces(info, choices, refs, cot_refs, sem)
        clear_spare(split)
        for piece in range(pieces):
            moves[piece].wait()
            fill_split(cot_refs.at[piece], split, piece * rows)
        keep = pltpu.make_async_copy(split, split_out, out_sem)
        keep.start()
        for b in range(width // BS):
            turned[b] = split[b].T

        def one(k):
            row, col = own_cell(own, 1, k)
            value = dot_plain(turned[col], hidden_ref[row])
            spread(out, k, value.T.astype(jnp.bfloat16), shares)

        each(total, one, 12)
        keep.wait()

    return stage(
        kernel, [hidden], refs,
        [
            (LOCAL, shape_of((shares, total, BS // shares, BS))),
            (pltpu.HBM, shape_of((width // BS + 1, all_rows, BS))),
        ],
        [
            pltpu.VMEM((pieces, rows, width), jnp.bfloat16),
            pltpu.VMEM((width // BS + 1, all_rows, BS), jnp.bfloat16),
            pltpu.VMEM((width // BS, BS, all_rows), jnp.bfloat16),
            pltpu.SemaphoreType.DMA((pieces,)),
            pltpu.SemaphoreType.DMA,
        ],
        operands, 2 * COST
    )


def up_grads_call(split, normed, slopes, width, shares, unloaded, operands):
    all_rows = split.shape[1]
    part_rows = all_rows // 2
    total = unloaded.shape[2]
    blocks = width // BS

    def kernel(layer, info, ins, results, scratch):
        sums, grad_pre, turned, *local, sem = scratch
        normed_ref, split_ref, blocks_here, slopes_ref = local
        out = results[0]
        sources = [ins[0], ins[1], ins[3].at[0, 1], ins[2]]
        moves = [
            pltpu.make_async_copy(source, target, sem.at[i])
            for i, (source, target) in enumerate(zip(sources, local))
        ]
        for move in moves:
            move.start()
        own = layer(OWN_LAYER)
        moves[0].wait()
        for b in range(blocks):
            turned[b] = normed_ref[b].T
        for move in moves[1:]:
            move.wait()

        def part_of(part):
            span = pl.ds(pl.multiple_of(part * part_rows, part_rows), part_rows)

            def finish(c, value):
                slope = slopes_ref[c, span, :].astype(jnp.float32)
                grad_pre[c, span, :] = (value * slope).astype(jnp.bfloat16)

            wide_pass(
                split_ref.at[:, span], blocks_here, own.lists, DOWN_WIDE, sums, finish, True, 4
            )

        each(2, part_of)

        def one(k):
            row, col = own_cell(own, 0, k)
            value = dot_plain(turned[row], grad_pre[col])
            spread(out, k, value.astype(jnp.bfloat16), shares)

        each(total, one, 4)

    return stage(
        kernel, [], [normed, split, slopes, unloaded],
        [(LOCAL, shape_of((shares, total, BS // shares, BS)))],
        [
            pltpu.VMEM((FF_BLOCKS, part_rows, BS), jnp.float32),
            pltpu.VMEM((FF_BLOCKS, all_rows, BS), jnp.bfloat16),
            pltpu.VMEM((blocks, BS, all_rows), jnp.bfloat16),
            pltpu.VMEM(normed.shape, normed.dtype),
            pltpu.VMEM(split.shape, split.dtype),
            pltpu.VMEM(unloaded.shape[2:], unloaded.dtype),
            pltpu.VMEM(slopes.shape, slopes.dtype),
            pltpu.SemaphoreType.DMA((4,)),
        ],
        operands, 4 * COST, OWN_VMEM
    )[0]


def adam_update(grad_sum, master, moment, variance, token_total):
    gradient = grad_sum / token_total
    moment_next = beta_first * moment + (1.0 - beta_first) * gradient
    variance_next = beta_second * variance + (1.0 - beta_second) * gradient * gradient
    corrected = moment_next / (1.0 - beta_first**update_count)
    spread = jnp.sqrt(variance_next / (1.0 - beta_second**update_count))
    step_direction = corrected / (spread + adam_eps)
    return (step_direction, master - learn_rate * (step_direction + decay_rate * master))


def shards(tokens, targets, weights, pattern, master, moment, variance):
    section = lax.axis_index("section")
    sections = lax.axis_size("section")
    shares = lax.axis_size("dp")
    groups = sections // 2
    micro, rows_each, width = tokens.shape[1:]
    rows = micro * rows_each
    half = rows // 2
    high = section >= groups
    high_member = high.astype(jnp.int32)
    group = jnp.minimum(section, sections - 1 - section)
    info = jnp.stack([high_member, 1 - high_member, jnp.zeros_like(high_member), high_member, group])
    far = lambda array: pltpu.with_memory_space_constraint(array, pltpu.HBM)
    tokens = far(tokens.reshape(2, rows, width))
    targets = far(targets.reshape(2, rows, width))
    pattern = pattern[0]
    lists = block_lists(pattern, width)
    mirror = lambda i: sections - 1 - i

    def lane(i, h):
        other = mirror(i + 1) if h else i + 1
        return [(i, other), (mirror(i), mirror(other))]

    def inward(x, i, h):
        return lax.ppermute(x, "section", lane(i, h))

    def outward(x, i, h):
        return lax.ppermute(x, "section", [(b, a) for a, b in lane(i, h)])

    def at_half(records, h, start=0):
        value = records[start][h]
        for i in range(start + 1, groups):
            value = jnp.where(group == i, records[i][h], value)
        return value

    def swap(low_records, high_records, h, sent):
        if sent is None:
            sent = jnp.where(high, at_half(low_records, h, 1), at_half(high_records, h))
        pairs = [(i, mirror(i)) for i in range(groups)] + [(mirror(i), i) for i in range(1, groups)]
        return lax.ppermute(sent, "section", pairs)

    halves = range(2)
    x_low, x_high, cot_low, cot_high = [[None] * groups for _ in range(4)]
    unloaded = far(weights[0])
    slope_low, slope_high = [[None] * groups for _ in range(2)]
    current = [enter_call(tokens, h, half, unloaded, (info, lists, None))[0] for h in halves]
    operands = (info, lists, weights[0])
    for i in range(groups - 1):
        current = [inward(current[h], i, h) for h in halves]
        x_low[i + 1] = current
        if i + 1 < groups - 1:
            moved = [forward_call(current[h], [LOW_LAYER], operands) for h in halves]
            current = [m[0] for m in moved]
            slope_low[i + 1] = [(far(m[1]), 0) for m in moved]
    both = [forward_call(current[h], [LOW_LAYER, HIGH_LAYER], operands) for h in halves]
    x_high[groups - 1] = [b[0] for b in both]
    slope_low[groups - 1] = [(far(b[2]), 0) for b in both]
    slope_high[groups - 1] = [(far(b[2]), 1) for b in both]
    current = [b[1] for b in both]
    for i in reversed(range(groups - 1)):
        current = [outward(current[h], i, h) for h in halves]
        x_high[i] = current
        if i > 0:
            moved = [forward_call(current[h], [HIGH_LAYER], operands) for h in halves]
            current = [m[0] for m in moved]
            slope_high[i] = [(far(m[1]), 0) for m in moved]
    mirrored = groups == 2
    entries = [x_high[0], x_high[1], x_low[1]] if mirrored else None
    turned = [turn_call(current[h], targets, h, operands, entries if h == 1 else None) for h in halves]
    cot_high[0] = [t[0] for t in turned]
    current = [t[1] for t in turned]
    for i in range(groups - 1):
        current = [inward(current[h], i, h) for h in halves]
        cot_high[i + 1] = current
        if i + 1 < groups - 1:
            current = [
                backward_call(
                    [x_high[i + 1][h]], [slope_high[i + 1][h]], current[h], [HIGH_LAYER], operands
                )[0]
                for h in halves
            ]
    last = groups - 1
    cot_sent = [None, None]
    cot_low[last], current, entering = [None, None], [None, None], current
    for h in halves:
        top, bottom = (x_high[last][h], x_low[last][h])
        tops, bottoms = slope_high[last][h], slope_low[last][h]
        sending = dict(turned=cot_high[0][h], last=last) if mirrored else {}
        if h == 0:
            moved = backward_call(
                [top, bottom], [tops, bottoms], entering[h], [HIGH_LAYER, LOW_LAYER], operands, **sending
            )
            cot_low[last][h], current[h], *sent = moved
        else:
            cot_low[last][h], *sent = backward_call(
                [top], [tops], entering[h], [HIGH_LAYER], operands, **sending
            )
            (current[h],) = backward_call(
                [bottom], [bottoms], cot_low[last][h], [LOW_LAYER], operands
            )
        cot_sent[h] = sent[0] if mirrored else None
    for i in reversed(range(1, last)):
        current = [outward(current[h], i, h) for h in halves]
        cot_low[i] = current
        current = [
            backward_call([x_low[i][h]], [slope_low[i][h]], current[h], [LOW_LAYER], operands)[0]
            for h in halves
        ]
    from_low = [lax.ppermute(current[h], "section", [(1, 0)]) for h in halves]
    from_high = [lax.ppermute(current[h], "section", [(mirror(1), 0)]) for h in halves]
    if mirrored:
        x_swapped = swap(None, None, None, turned[1][2])
        x_other = [(x_swapped, pl.ds(h * half, half)) for h in halves]
    else:
        x_other = [(swap(x_low, x_high, h, None), None) for h in halves]
    cot_other = []
    for h in halves:
        cot_other.append((swap(cot_low, cot_high, h, cot_sent[h]), None))

    def choose(low_records, high_records, others, first_own, first_other):
        refs, choices = [], []

        def add(array):
            refs.append(array)
            return len(refs) - 1

        for h in halves:
            array, index = first_own[h]
            options = [("first", None, add(array), index)]
            for i in range(groups):
                if i > 0:
                    options.append(("own", (0, i), add(low_records[i][h]), None))
                options.append(("own", (1, i), add(high_records[i][h]), None))
            choices.append(options)
        for h in halves:
            array, index = first_other[h]
            choices.append([("first", None, add(array), index), ("rest", None, add(others[h][0]), others[h][1])])
        return refs, choices

    def token_piece(member, h):
        return (tokens, (member, pl.ds(h * half, half)))

    refs, choices = choose(
        x_low, x_high, x_other, [token_piece(0, h) for h in halves], [token_piece(1, h) for h in halves]
    )
    hidden, slopes, normed = ups_call(refs, choices, current[1], half, width, unloaded, (info, lists, None))
    refs, choices = choose(
        cot_low, cot_high, cot_other,
        [(from_low[0], None), (from_high[1], None)], [(from_high[0], None), (from_low[1], None)]
    )
    downs, split = down_grads_call(
        refs, choices, hidden, half, width, shares, unloaded.shape[2], (info, lists, None)
    )

    def reduce(grads):
        return lax.psum_scatter(grads, "dp", scatter_dimension=0, tiled=True)[0].astype(jnp.float32)

    down_share = reduce(downs)
    up_share = reduce(up_grads_call(far(split), far(normed), far(slopes), width, shares, unloaded, (info, lists, None)))
    token_total = 2 * rows * shares
    step_direction, master_next = adam_update(
        jnp.stack([down_share, up_share])[::-1], master[0], moment[0], variance[0], token_total
    )
    return (step_direction[None], master_next[None])


def solution(mesh):
    rows_split = P(None, None, "dp", None)
    by_section = P("section", None, None, "dp", None)
    return jax.shard_map(
        shards,
        mesh=mesh,
        in_specs=(
            rows_split,
            rows_split,
            P("section", None, None, None, None, None),
            P("section", None, None, None, None),
            by_section,
            by_section,
            by_section,
        ),
        out_specs=(by_section, by_section),
        check_vma=False,
    )
```

profile of v0, /device:TPU:0, one launch (start us, length us, event | category | flops | bytes accessed | tf_op | source)
XLA Modules:
  0.0 274.6 jit_solution(13401341545162987595)
XLA Ops:
  7.2 0.7 slice.20
  7.9 0.7 copy.58
  8.7 0.4 convert_reduce_fusion.2
  9.1 0.2 convert_reduce_fusion.3
  9.2 0.1 copy.56
  9.3 0.1 copy.55
  9.5 0.1 copy.53
  9.6 0.5 convert_reduce_fusion
  10.3 0.1 constant_dynamic-update-slice_fusion.4
  10.4 0.1 constant_dynamic-update-slice_fusion.2
  10.5 0.1 constant_dynamic-update-slice_fusion.12
  10.6 0.1 constant_dynamic-update-slice_fusion.9
  10.7 1.2 select_reduce_fusion
  12.1 0.1 reshape.404
  12.2 0.1 copy.54
  12.3 0.1 reshape_squeeze.3
  12.5 0.1 stack.59.info_ref
  12.6 7.8 %shard_map.86 = bf16[112,2048]{1,0:T(8,128)(2,1)S(1)} custom-call(s32[5]{0:T(128)S(1)} %stack.59.info_ref, s32[7296]{0:T(1024)S(1)} %constant_dynamic-update-slice_fusion.17.lists_ref, bf16[2,224,2048]{2,1,0:T(8,128)(2,1)} %bitcast.140, bf16[2,2,96,128,128]{4,3,2,1,0:T(8,128)(2,1)} %bitcast.127), custom_call_target="tpu_custom_call" | custom-call | flops 4000000000 | tf_op jit(solution)/shard_map/pallas_call | solution.py:265
  20.4 5.4 %collective-permute-start = (bf16[112,2048]{1,0:T(8,128)(2,1)S(1)}, bf16[112,2048]{1,0:T(8,128)(2,1)S(1)}, u32[]{:S(2)}, u32[]{:S(2)}) collective-permute-start(bf16[112,2048]{1,0:T(8,128)(2,1)S(1)} %shard_map.86), channel_id=1, source_target_pairs={{0,8},{24,16},{1,9},{25,17},{2,10},{26,18},{3,11},{27,19},{4,12},{... | collective-permute-start | bytes 1376264 | tf_op jit(solution)/shard_map/ppermute | solution.py:683
  25.8 7.3 %shard_map.88 = bf16[112,2048]{1,0:T(8,128)(2,1)S(1)} custom-call(s32[5]{0:T(128)S(1)} %stack.59.info_ref, s32[7296]{0:T(1024)S(1)} %constant_dynamic-update-slice_fusion.17.lists_ref, bf16[2,224,2048]{2,1,0:T(8,128)(2,1)} %bitcast.141, bf16[2,2,96,128,128]{4,3,2,1,0:T(8,128)(2,1)} %bitcast.128), custom_call_target="tpu_custom_call" | custom-call | flops 4000000000 | tf_op jit(solution)/shard_map/pallas_call | solution.py:265
  33.1 1.5 collective-permute-start.2
  34.7 0.9 collective-permute-done.rest_1_.rest_6_.rest_2_
  35.5 11.7 %shard_map.87 = (bf16[112,2048]{1,0:T(8,128)(2,1)S(1)}, bf16[112,2048]{1,0:T(8,128)(2,1)S(1)}, bf16[2,64,112,128]{3,2,1,0:T(8,128)(2,1)}) custom-call(s32[5]{0:T(128)S(1)} %stack.59.info_ref, s32[7296]{0:T(1024)S(1)} %constant_dynamic-update-slice_fusion.17.lists_ref, bf16[2,2,96,128,128]{4,3,2,1,0:T(8,128)(2,1)S(1)} %bitcast.133, ...), custom_call_target="tpu_custom_call" | custom-call | flops 8000000000 | tf_op jit(solution)/shard_map/pallas_call | solution.py:265
  47.3 1.3 collective-permute-start.1
  48.6 11.9 %shard_map.89 = (bf16[112,2048]{1,0:T(8,128)(2,1)S(1)}, bf16[112,2048]{1,0:T(8,128)(2,1)S(1)}, bf16[2,64,112,128]{3,2,1,0:T(8,128)(2,1)}) custom-call(s32[5]{0:T(128)S(1)} %stack.59.info_ref, s32[7296]{0:T(1024)S(1)} %constant_dynamic-update-slice_fusion.17.lists_ref, bf16[2,2,96,128,128]{4,3,2,1,0:T(8,128)(2,1)S(1)} %bitcast.134, ...), custom_call_target="tpu_custom_call" | custom-call | flops 8000000000 | tf_op jit(solution)/shard_map/pallas_call | solution.py:265
  60.5 1.3 collective-permute-start.3
  61.8 11.5 %shard_map.94 = (bf16[112,2048]{1,0:T(8,128)(2,1)S(1)}, bf16[112,2048]{1,0:T(8,128)(2,1)S(1)}) custom-call(s32[5]{0:T(128)S(1)} %stack.59.info_ref, s32[7296]{0:T(1024)S(1)} %constant_dynamic-update-slice_fusion.17.lists_ref, bf16[2,2,96,128,128]{4,3,2,1,0:T(8,128)(2,1)S(1)} %bitcast.135, bf16[112,2048]{1,0:T(8,128)(2,1)S(1)} %collective-permute-done.1.rest_2_.rest_1_, ...), custom_call_target="tpu_custom_call" | custom-call | flops 12000000000 | tf_op jit(solution)/shard_map/pallas_call | solution.py:265
  73.3 5.1 %collective-permute-start.6 = (bf16[112,2048]{1,0:T(8,128)(2,1)S(1)}, bf16[112,2048]{1,0:T(8,128)(2,1)S(1)}, u32[]{:S(2)}, u32[]{:S(2)}) collective-permute-start(bf16[112,2048]{1,0:T(8,128)(2,1)S(1)} %get-tuple-element.33), channel_id=1, source_target_pairs={{0,8},{24,16},{1,9},{25,17},{2,10},{26,18},{3,11},{27,19},{4,12},{... | collective-permute-start | bytes 1376264 | tf_op jit(solution)/shard_map/ppermute | solution.py:683
  78.5 11.6 %shard_map.90 = (bf16[112,2048]{1,0:T(8,128)(2,1)S(1)}, bf16[112,2048]{1,0:T(8,128)(2,1)S(1)}, bf16[224,2048]{1,0:T(8,128)(2,1)S(1)}) custom-call(s32[5]{0:T(128)S(1)} %stack.59.info_ref, s32[7296]{0:T(1024)S(1)} %constant_dynamic-update-slice_fusion.17.lists_ref, bf16[2,2,96,128,128]{4,3,2,1,0:T(8,128)(2,1)S(1)} %bitcast.136, ...), custom_call_target="tpu_custom_call" | custom-call | flops 12000000000 | tf_op jit(solution)/shard_map/pallas_call | solution.py:265
  90.1 1.3 collective-permute-start.5
  91.4 3.5 %collective-permute-start.4 = (bf16[224,2048]{1,0:T(8,128)(2,1)S(1)}, bf16[224,2048]{1,0:T(8,128)(2,1)S(1)}, u32[]{:S(2)}, u32[]{:S(2)}) collective-permute-start(bf16[224,2048]{1,0:T(8,128)(2,1)S(1)} %get-tuple-element.27), channel_id=1, source_target_pairs={{0,24},{8,16},{16,8},{1,25},{9,17},{17,9},{2,26},{10,18},{18,10},{... | collective-permute-start | bytes 2752520 | tf_op jit(solution)/shard_map/ppermute | solution.py:698
  94.9 12.5 %shard_map.95 = (bf16[112,2048]{1,0:T(8,128)(2,1)S(1)}, bf16[112,2048]{1,0:T(8,128)(2,1)S(1)}, bf16[112,2048]{1,0:T(8,128)(2,1)S(1)}) custom-call(s32[5]{0:T(128)S(1)} %stack.59.info_ref, s32[7296]{0:T(1024)S(1)} %constant_dynamic-update-slice_fusion.17.lists_ref, bf16[2,2,96,128,128]{4,3,2,1,0:T(8,128)(2,1)S(1)} %bitcast.137, ...), custom_call_target="tpu_custom_call" | custom-call | flops 16000000000 | tf_op jit(solution)/shard_map/pallas_call | solution.py:265
  107.4 1.3 collective-permute-start.9
  108.7 1.3 collective-permute-start.7
  110.0 1.3 collective-permute-start.10
  111.3 8.6 %collective-permute-done.5.rest_2_.rest_8_ = bf16[112,2048]{1,0:T(8,128)(2,1)S(1)} collective-permute-done((bf16[112,2048]{1,0:T(8,128)(2,1)S(1)}, bf16[112,2048]{1,0:T(8,128)(2,1)S(1)}, u32[]{:S(2)}, u32[]{:S(2)}) %collective-permute-start.5) | collective-permute-done | bytes 458784 | tf_op jit(solution)/shard_map/ppermute | solution.py:683
  119.9 7.5 %shard_map.91 = (bf16[112,2048]{1,0:T(8,128)(2,1)S(1)}, bf16[112,2048]{1,0:T(8,128)(2,1)S(1)}) custom-call(s32[5]{0:T(128)S(1)} %stack.59.info_ref, s32[7296]{0:T(1024)S(1)} %constant_dynamic-update-slice_fusion.17.lists_ref, bf16[2,2,96,128,128]{4,3,2,1,0:T(8,128)(2,1)S(1)} %bitcast.138, bf16[112,2048]{1,0:T(8,128)(2,1)S(1)} %get-tuple-element.26.rest_5_.rest_1_.rest_7_, ...), custom_call_target="tpu_custom_call" | custom-call | flops 8000000000 | tf_op jit(solution)/shard_map/pallas_call | solution.py:265
  127.5 7.5 %shard_map.92.rest_12_ = bf16[112,2048]{1,0:T(8,128)(2,1)S(1)} custom-call(s32[5]{0:T(128)S(1)} %stack.59.info_ref, s32[7296]{0:T(1024)S(1)} %constant_dynamic-update-slice_fusion.17.lists_ref, bf16[2,2,96,128,128]{4,3,2,1,0:T(8,128)(2,1)S(1)} %bitcast.139, bf16[112,2048]{1,0:T(8,128)(2,1)S(1)} %collective-permute-done.2.rest_1_.rest_7_.rest_6_, ...), custom_call_target="tpu_custom_call" | custom-call | flops 8000000000 | tf_op jit(solution)/shard_map/pallas_call | solution.py:265
  135.0 1.3 collective-permute-start.11
  136.3 1.5 collective-permute-start.8
  137.8 12.1 %collective-permute-start.12 = (bf16[112,2048]{1,0:T(8,128)(2,1)S(1)}, bf16[112,2048]{1,0:T(8,128)(2,1)S(1)}, u32[]{:S(2)}, u32[]{:S(2)}) collective-permute-start(bf16[112,2048]{1,0:T(8,128)(2,1)S(1)} %get-tuple-element.39), channel_id=1, source_target_pairs={{0,24},{8,16},{16,8},{1,25},{9,17},{17,9},{2,26},{10,18},{18,10},{... | collective-permute-start | bytes 1376264 | tf_op jit(solution)/shard_map/ppermute | solution.py:698
  149.9 18.6 %shard_map.93 = (bf16[64,448,128]{2,1,0:T(8,128)(2,1)S(1)}, bf16[64,448,128]{2,1,0:T(8,128)(2,1)}, bf16[17,448,128]{2,1,0:T(8,128)(2,1)}) custom-call(s32[5]{0:T(128)S(1)} %stack.59.info_ref, s32[7296]{0:T(1024)S(1)} %constant_dynamic-update-slice_fusion.17.lists_ref, bf16[2,224,2048]{2,1,0:T(8,128)(2,1)} %bitcast.142, ...), custom_call_target="tpu_custom_call" | custom-call | flops 16000000000 | tf_op jit(solution)/shard_map/pallas_call | solution.py:265
  168.5 10.2 %shard_map.96 = (bf16[8,96,16,128]{3,2,1,0:T(8,128)(2,1)}, bf16[17,448,128]{2,1,0:T(8,128)(2,1)}) custom-call(s32[5]{0:T(128)S(1)} %stack.59.info_ref, s32[7296]{0:T(1024)S(1)} %constant_dynamic-update-slice_fusion.17.lists_ref, bf16[64,448,128]{2,1,0:T(8,128)(2,1)S(1)} %get-tuple-element.32.rest_0_, bf16[112,2048]{1,0:T(8,128)(2,1)S(1)} %collective-permute-done.7.rest_1_, ...), custom_call_target="tpu_custom_call" | custom-call | flops 8000000000 | tf_op jit(solution)/shard_map/pallas_call | solution.py:265
  178.8 25.4 %shard_map.97 = bf16[8,96,16,128]{3,2,1,0:T(8,128)(2,1)} custom-call(s32[5]{0:T(128)S(1)} %stack.59.info_ref, s32[7296]{0:T(1024)S(1)} %constant_dynamic-update-slice_fusion.17.lists_ref, bf16[17,448,128]{2,1,0:T(8,128)(2,1)} %get-tuple-element.41.rest_0_, bf16[17,448,128]{2,1,0:T(8,128)(2,1)} %get-tuple-element.42.rest_1_, ...), custom_call_target="tpu_custom_call" | custom-call | flops 16000000000 | tf_op jit(solution)/shard_map/pallas_call | solution.py:265
  204.2 15.9 %reduce-scatter.3.cloned.1.call-done = bf16[1,96,16,128]{3,2,1,0:T(8,128)(2,1)} async-done(((bf16[8,96,16,128]{3,2,1,0:T(8,128)(2,1)}), bf16[1,96,16,128]{3,2,1,0:T(8,128)(2,1)}) %reduce-scatter.3.cloned.1.call-update) | async-done | bytes 393232 | tf_op jit(solution)/shard_map/reduce_scatter | solution.py:814
  220.1 42.1 %reduce-scatter.5.cloned.1.call-done = bf16[1,96,16,128]{3,2,1,0:T(8,128)(2,1)} async-done(((bf16[8,96,16,128]{3,2,1,0:T(8,128)(2,1)}), bf16[1,96,16,128]{3,2,1,0:T(8,128)(2,1)}) %reduce-scatter.5.cloned.1.call-update) | async-done | bytes 393232 | tf_op jit(solution)/shard_map/reduce_scatter | solution.py:814
  262.2 1.2 maximum_convert_fusion
  263.4 4.3 %fusion.2 = (f32[1,2,96,16,128]{4,3,2,1,0:T(8,128)}, f32[2,96,16,128]{3,2,1,0:T(8,128)}) fusion(f32[1,2,96,16,128]{4,3,2,1,0:T(8,128)S(1)} %copy-done, f32[1,2,96,16,128]{4,3,2,1,0:T(8,128)S(1)} %copy-done.1, f32[2,96,16,128]{3,2,1,0:T(8,128)S(1)} %maximum_convert_fusion, f32[1,2,96,16,128]{4,3,2,1,0:T(8,128)} %param.12), kind=kLoop, calls=%fused_computation.6 | loop fusion | flops 6291456 | bytes 9437184 | tf_op jit(solution)/shard_map/broadcast_in_dim | solution.py:822
  (53 shorter events, 0.8 us)
Async XLA Ops:
  7.2 213.0 %reduce-scatter.3.cloned.1.call-start = ((), (), s32[]{:S(2)}) async-start(), calls=%async_computation.2 | async-start | bytes 3538944 | tf_op jit(solution)/shard_map/reduce_scatter | solution.py:814
  12.6 22.9 %slice-start = ((s8[12582912]{0:T(1024)(128)(4,1)}), s8[4194304]{0:T(1024)(128)(4,1)S(1)}, s32[]{:S(2)}) async-start(s8[12582912]{0:T(1024)(128)(4,1)} %bitcast.131), calls=%async_computation.4 | async-start | bytes 8388608
  12.6 22.9 %slice-start.1 = ((s8[12582912]{0:T(1024)(128)(4,1)}), s8[4194304]{0:T(1024)(128)(4,1)S(1)}, s32[]{:S(2)}) async-start(s8[12582912]{0:T(1024)(128)(4,1)} %bitcast.131), calls=%async_computation.5 | async-start | bytes 8388608
  20.4 15.2 %slice-start.2 = ((s8[12582912]{0:T(1024)(128)(4,1)}), s8[4194304]{0:T(1024)(128)(4,1)S(1)}, s32[]{:S(2)}) async-start(s8[12582912]{0:T(1024)(128)(4,1)} %bitcast.131), calls=%async_computation.6 | async-start | bytes 8388608
  20.4 15.1 %collective-permute-start = (bf16[112,2048]{1,0:T(8,128)(2,1)S(1)}, bf16[112,2048]{1,0:T(8,128)(2,1)S(1)}, u32[]{:S(2)}, u32[]{:S(2)}) collective-permute-start(bf16[112,2048]{1,0:T(8,128)(2,1)S(1)} %shard_map.86), channel_id=1, source_target_pairs={{0,8},{24,16},{1,9},{25,17},{2,10},{26,18},{3,11},{27,19},{4,12},{... | collective-permute-start | bytes 1376264 | tf_op jit(solution)/shard_map/ppermute | solution.py:683
  33.1 15.5 %collective-permute-start.2 = (bf16[112,2048]{1,0:T(8,128)(2,1)S(1)}, bf16[112,2048]{1,0:T(8,128)(2,1)S(1)}, u32[]{:S(2)}, u32[]{:S(2)}) collective-permute-start(bf16[112,2048]{1,0:T(8,128)(2,1)S(1)} %shard_map.88), channel_id=1, source_target_pairs={{0,16},{24,8},{1,17},{25,9},{2,18},{26,10},{3,19},{27,11},{4,20},{... | collective-permute-start | bytes 1376264 | tf_op jit(solution)/shard_map/ppermute | solution.py:683
  47.3 14.5 %collective-permute-start.1 = (bf16[112,2048]{1,0:T(8,128)(2,1)S(1)}, bf16[112,2048]{1,0:T(8,128)(2,1)S(1)}, u32[]{:S(2)}, u32[]{:S(2)}) collective-permute-start(bf16[112,2048]{1,0:T(8,128)(2,1)S(1)} %get-tuple-element.23), channel_id=1, source_target_pairs={{8,0},{16,24},{9,1},{17,25},{10,2},{18,26},{11,3},{19,27},{12,4},{... | collective-permute-start | bytes 1376264 | tf_op jit(solution)/shard_map/ppermute | solution.py:686
  60.5 18.0 %collective-permute-start.3 = (bf16[112,2048]{1,0:T(8,128)(2,1)S(1)}, bf16[112,2048]{1,0:T(8,128)(2,1)S(1)}, u32[]{:S(2)}, u32[]{:S(2)}) collective-permute-start(bf16[112,2048]{1,0:T(8,128)(2,1)S(1)} %get-tuple-element.25), channel_id=1, source_target_pairs={{16,0},{8,24},{17,1},{9,25},{18,2},{10,26},{19,3},{11,27},{20,4},{... | collective-permute-start | bytes 1376264 | tf_op jit(solution)/shard_map/ppermute | solution.py:686
  73.3 21.5 %collective-permute-start.6 = (bf16[112,2048]{1,0:T(8,128)(2,1)S(1)}, bf16[112,2048]{1,0:T(8,128)(2,1)S(1)}, u32[]{:S(2)}, u32[]{:S(2)}) collective-permute-start(bf16[112,2048]{1,0:T(8,128)(2,1)S(1)} %get-tuple-element.33), channel_id=1, source_target_pairs={{0,8},{24,16},{1,9},{25,17},{2,10},{26,18},{3,11},{27,19},{4,12},{... | collective-permute-start | bytes 1376264 | tf_op jit(solution)/shard_map/ppermute | solution.py:683
  90.1 29.9 %collective-permute-start.5 = (bf16[112,2048]{1,0:T(8,128)(2,1)S(1)}, bf16[112,2048]{1,0:T(8,128)(2,1)S(1)}, u32[]{:S(2)}, u32[]{:S(2)}) collective-permute-start(bf16[112,2048]{1,0:T(8,128)(2,1)S(1)} %get-tuple-element.28), channel_id=1, source_target_pairs={{0,16},{24,8},{1,17},{25,9},{2,18},{26,10},{3,19},{27,11},{4,20},{... | collective-permute-start | bytes 1376264 | tf_op jit(solution)/shard_map/ppermute | solution.py:683
  91.4 46.4 %collective-permute-start.4 = (bf16[224,2048]{1,0:T(8,128)(2,1)S(1)}, bf16[224,2048]{1,0:T(8,128)(2,1)S(1)}, u32[]{:S(2)}, u32[]{:S(2)}) collective-permute-start(bf16[224,2048]{1,0:T(8,128)(2,1)S(1)} %get-tuple-element.27), channel_id=1, source_target_pairs={{0,24},{8,16},{16,8},{1,25},{9,17},{17,9},{2,26},{10,18},{18,10},{... | collective-permute-start | bytes 2752520 | tf_op jit(solution)/shard_map/ppermute | solution.py:698
  107.4 61.0 %collective-permute-start.9 = (bf16[112,2048]{1,0:T(8,128)(2,1)S(1)}, bf16[112,2048]{1,0:T(8,128)(2,1)S(1)}, u32[]{:S(2)}, u32[]{:S(2)}) collective-permute-start(bf16[112,2048]{1,0:T(8,128)(2,1)S(1)} %get-tuple-element.36), channel_id=1, source_target_pairs={{16,0},{17,1},{18,2},{19,3},{20,4},{21,5},{22,6},{23,7}} | collective-permute-start | bytes 1376264 | tf_op jit(solution)/shard_map/ppermute | solution.py:768
  108.7 59.7 %collective-permute-start.7 = (bf16[112,2048]{1,0:T(8,128)(2,1)S(1)}, bf16[112,2048]{1,0:T(8,128)(2,1)S(1)}, u32[]{:S(2)}, u32[]{:S(2)}) collective-permute-start(bf16[112,2048]{1,0:T(8,128)(2,1)S(1)} %get-tuple-element.36), channel_id=1, source_target_pairs={{8,0},{9,1},{10,2},{11,3},{12,4},{13,5},{14,6},{15,7}} | collective-permute-start | bytes 1376264 | tf_op jit(solution)/shard_map/ppermute | solution.py:767
  110.0 26.3 %collective-permute-start.10 = (bf16[112,2048]{1,0:T(8,128)(2,1)S(1)}, bf16[112,2048]{1,0:T(8,128)(2,1)S(1)}, u32[]{:S(2)}, u32[]{:S(2)}) collective-permute-start(bf16[112,2048]{1,0:T(8,128)(2,1)S(1)} %get-tuple-element.38), channel_id=1, source_target_pairs={{0,24},{8,16},{16,8},{1,25},{9,17},{17,9},{2,26},{10,18},{18,10},{... | collective-permute-start | bytes 1376264 | tf_op jit(solution)/shard_map/ppermute | solution.py:698
  135.0 33.5 %collective-permute-start.11 = (bf16[112,2048]{1,0:T(8,128)(2,1)S(1)}, bf16[112,2048]{1,0:T(8,128)(2,1)S(1)}, u32[]{:S(2)}, u32[]{:S(2)}) collective-permute-start(bf16[112,2048]{1,0:T(8,128)(2,1)S(1)} %shard_map.92.rest_12_), channel_id=1, source_target_pairs={{8,0},{9,1},{10,2},{11,3},{12,4},{13,5},{14,6},{15,7}} | collective-permute-start | bytes 1376264 | tf_op jit(solution)/shard_map/ppermute | solution.py:767
  136.3 32.2 %collective-permute-start.8 = (bf16[112,2048]{1,0:T(8,128)(2,1)S(1)}, bf16[112,2048]{1,0:T(8,128)(2,1)S(1)}, u32[]{:S(2)}, u32[]{:S(2)}) collective-permute-start(bf16[112,2048]{1,0:T(8,128)(2,1)S(1)} %shard_map.92.rest_12_), channel_id=1, source_target_pairs={{16,0},{17,1},{18,2},{19,3},{20,4},{21,5},{22,6},{23,7}} | collective-permute-start | bytes 1376264 | tf_op jit(solution)/shard_map/ppermute | solution.py:768
  137.8 30.7 %collective-permute-start.12 = (bf16[112,2048]{1,0:T(8,128)(2,1)S(1)}, bf16[112,2048]{1,0:T(8,128)(2,1)S(1)}, u32[]{:S(2)}, u32[]{:S(2)}) collective-permute-start(bf16[112,2048]{1,0:T(8,128)(2,1)S(1)} %get-tuple-element.39), channel_id=1, source_target_pairs={{0,24},{8,16},{16,8},{1,25},{9,17},{17,9},{2,26},{10,18},{18,10},{... | collective-permute-start | bytes 1376264 | tf_op jit(solution)/shard_map/ppermute | solution.py:698
  178.8 83.5 %reduce-scatter.5.cloned.1.call-start = ((), (), s32[]{:S(2)}) async-start(), calls=%async_computation.3 | async-start | bytes 3538944 | tf_op jit(solution)/shard_map/reduce_scatter | solution.py:814
  204.2 59.2 %copy-start.1 = (f32[1,2,96,16,128]{4,3,2,1,0:T(8,128)S(1)}, f32[1,2,96,16,128]{4,3,2,1,0:T(8,128)}, u32[]{:S(2)}) copy-start(f32[1,2,96,16,128]{4,3,2,1,0:T(8,128)} %param.13) | copy-start | bytes 4718596
  204.2 59.2 %copy-start = (f32[1,2,96,16,128]{4,3,2,1,0:T(8,128)S(1)}, f32[1,2,96,16,128]{4,3,2,1,0:T(8,128)}, u32[]{:S(2)}) copy-start(f32[1,2,96,16,128]{4,3,2,1,0:T(8,128)} %param.11) | copy-start | bytes 4718596
Sparse Core Ops, SparseCore 0:
  178.9 41.2 reduce-scatter.2
  222.4 39.7 reduce-scatter.4
where the time goes:
time: 275 us
  Pallas kernels  144 us (52%)
  waiting for transfers between devices  67.5 us (25%)
  starting transfers between devices  38.3 us (14%)
  between operations  14.5 us (5%)
  other arithmetic  8.53 us (3%)
    pallas_call x12, Pallas kernels, stage(): pl.pallas_call(body, in_specs=[smem_spec, smem_spec] + [vmem_spec] * (len...  144 us
    reduce_scatter x2, waiting for transfers between devices, reduce(): lax.psum_scatter(grads, 'dp', scatter_dimension=0, tiled=True)[0]  58 us
    ppermute x3, starting transfers between devices, swap(): return lax.ppermute(sent, 'section', pairs)  16.8 us
    ppermute x4, starting transfers between devices, inward(): return lax.ppermute(x, 'section', lane(i, h))  13.4 us
    ppermute x4, waiting for transfers between devices, inward(): return lax.ppermute(x, 'section', lane(i, h))  9.45 us
  transfers between devices with their start and end apart: 15, of which 4 were waited for; matrix products, arithmetic and copies ran while one was open for 0% of the time, Pallas kernels for 46%

commit v1 on v0

--- a/solution.py
+++ b/solution.py
@@ -359,9 +359,8 @@
     return stage(kernel, [], [tokens, unloaded], outs, scratch, operands, COST * ENTER_COST, CHAIN_VMEM)
 
 
-def turn_call(x, targets, h, operands, entries=None):
+def turn_call(x, targets, h, operands):
     rows, width = x.shape
-    local = [x] + ([] if entries is None else [e for pair in entries for e in pair])
 
     def kernel(layer, info, ins, results, scratch):
         *layer_refs, slopes, aim, sem = scratch
@@ -378,18 +377,9 @@
             difference = residue[:, cols].astype(jnp.float32) - aim[:, cols].astype(jnp.float32)
             residue[:, cols] = difference.astype(jnp.bfloat16)
         backward_rows(x_ref, residue, out, own, layer_refs, slopes)
-        if entries is not None:
-            high, group = info[HIGH] == 1, info[GROUP]
-            conditions = [~high & (group == 0), ~high & (group != 0), high]
-            for i in range(2):
-                sources = [ins[1 + 2 * j + i] for j in range(3)]
-                pick_rows(results[2].at[pl.ds(i * rows, rows)], list(zip(conditions, sources)))
-
-    outs = [(LOCAL, shape_of(x.shape))] * 2
-    if entries is not None:
-        outs.append((LOCAL, shape_of((2 * rows, width))))
+
     return stage(
-        kernel, local, [targets], outs,
+        kernel, [x], [targets], [(LOCAL, shape_of(x.shape))] * 2,
         layer_scratch(rows, width) + slope_scratch(rows)
         + [pltpu.VMEM((rows, width), jnp.bfloat16), pltpu.SemaphoreType.DMA],
         operands, 3 * COST
@@ -404,10 +394,10 @@
             target[...] = source[...]
 
 
-def backward_call(xs, saved, cot, whichs, operands, turned=None, last=None):
+def backward_call(xs, saved, cot, whichs, operands, turned=None, last=None, entries=()):
     rows, width = cot.shape
     steps = len(whichs)
-    local = list(xs) + [cot] + ([] if turned is None else [turned])
+    local = list(xs) + [cot] + ([] if turned is None else [turned]) + list(entries)
 
     def kernel(layer, info, ins, results, scratch):
         *layer_refs, slopes, sem = scratch
@@ -434,12 +424,15 @@
                     (~high & (group != last), ins[steps + 1]),
                 ],
             )
+        if entries:
+            conditions = [~high & (group != last), ~high & (group == last), high]
+            pick_rows(results[steps + 1], list(zip(conditions, ins[steps + 2 :])))
 
     scratch = [
         pltpu.VMEM((steps, FF_BLOCKS, rows, BS), jnp.bfloat16),
         pltpu.SemaphoreType.DMA((steps,)),
     ]
-    outs = [(LOCAL, shape_of(cot.shape))] * (steps + (turned is not None))
+    outs = [(LOCAL, shape_of(cot.shape))] * (steps + (turned is not None) + bool(entries))
     return stage(
         kernel, local, [array for array, _ in saved], outs, layer_scratch(rows, width) + scratch,
         operands, 2 * COST * steps
@@ -723,8 +716,9 @@
             current = [m[0] for m in moved]
             slope_high[i] = [(far(m[1]), 0) for m in moved]
     mirrored = groups == 2
-    entries = [x_high[0], x_high[1], x_low[1]] if mirrored else None
-    turned = [turn_call(current[h], targets, h, operands, entries if h == 1 else None) for h in halves]
+    turned = []
+    for h in halves:
+        turned.append(turn_call(current[h], targets, h, operands))
     cot_high[0] = [t[0] for t in turned]
     current = [t[1] for t in turned]
     for i in range(groups - 1):
@@ -745,10 +739,13 @@
         tops, bottoms = slope_high[last][h], slope_low[last][h]
         sending = dict(turned=cot_high[0][h], last=last) if mirrored else {}
         if h == 0:
+            if mirrored:
+                sending["entries"] = [x_high[0][1], x_high[1][1], x_low[1][1]]
             moved = backward_call(
                 [top, bottom], [tops, bottoms], entering[h], [HIGH_LAYER, LOW_LAYER], operands, **sending
             )
             cot_low[last][h], current[h], *sent = moved
+            x_sent = sent[1] if mirrored else None
         else:
             cot_low[last][h], *sent = backward_call(
                 [top], [tops], entering[h], [HIGH_LAYER], operands, **sending
@@ -764,13 +761,13 @@
             backward_call([x_low[i][h]], [slope_low[i][h]], current[h], [LOW_LAYER], operands)[0]
             for h in halves
         ]
-    from_low = [lax.ppermute(current[h], "section", [(1, 0)]) for h in halves]
-    from_high = [lax.ppermute(current[h], "section", [(mirror(1), 0)]) for h in halves]
-    if mirrored:
-        x_swapped = swap(None, None, None, turned[1][2])
-        x_other = [(x_swapped, pl.ds(h * half, half)) for h in halves]
-    else:
-        x_other = [(swap(x_low, x_high, h, None), None) for h in halves]
+    from_low, from_high = [], []
+    for h in halves:
+        from_low.append(lax.ppermute(current[h], "section", [(1, 0)]))
+        from_high.append(lax.ppermute(current[h], "section", [(mirror(1), 0)]))
+    x_other = []
+    for h in halves:
+        x_other.append((swap(x_low, x_high, h, x_sent if h else None), None))
     cot_other = []
     for h in halves:
         cot_other.append((swap(cot_low, cot_high, h, cot_sent[h]), None))

time: 275 us -> 274 us (level)
  starting transfers between devices: 38.3 us -> 30.5 us
  local copies, waits for them, and re-layouts: 2.28 us -> 6.84 us
    ppermute x3 -> x4, starting transfers between devices: 16.8 us -> 9.36 us  [swap(): return lax.ppermute(sent, 'section', pairs)]
    reduce_scatter x2, waiting for transfers between devices: 58 us -> 64.8 us  [reduce(): lax.psum_scatter(grads, 'dp', scatter_dimension=0, tiled=True)[0]]
    ppermute x4, waiting for transfers between devices: 9.45 us -> 3.29 us  [inward(): return lax.ppermute(x, 'section', lane(i, h))]
    unnamed x20 -> x16, local copies, waits for them, and re-layouts: 0.96 us -> 5.52 us
  transfers between devices with their start and end apart: 15 -> 16, of which waited for: 4 -> 5; matrix products, arithmetic and copies ran while one was open for 0% -> 0% of each run, Pallas kernels for 46% -> 46%
where the time goes in v1:
time: 274 us
  Pallas kernels  143 us (52%)
  waiting for transfers between devices  70.2 us (26%)
  starting transfers between devices  30.5 us (11%)
  between operations  14.5 us (5%)
  other arithmetic  8.65 us (3%)
  local copies, waits for them, and re-layouts  6.84 us (2%)
    pallas_call x12, Pallas kernels, stage(): pl.pallas_call(body, in_specs=[smem_spec, smem_spec] + [vmem_spec] * (len...  143 us
    reduce_scatter x2, waiting for transfers between devices, reduce(): lax.psum_scatter(grads, 'dp', scatter_dimension=0, tiled=True)[0]  64.8 us
    ppermute x4, starting transfers between devices, inward(): return lax.ppermute(x, 'section', lane(i, h))  13.1 us
    ppermute x4, starting transfers between devices, swap(): return lax.ppermute(sent, 'section', pairs)  9.36 us
    unnamed x16, local copies, waits for them, and re-layouts  5.52 us
  transfers between devices with their start and end apart: 16, of which 5 were waited for; matrix products, arithmetic and copies ran while one was open for 0% of the time, Pallas kernels for 46%

profile of v1, /device:TPU:0, one launch (start us, length us, event | category | flops | bytes accessed | tf_op | source)
XLA Modules:
  0.0 273.8 jit_solution(5381006260485650452)
XLA Ops:
  7.2 0.7 slice.20
  7.9 0.7 copy.58
  8.7 0.4 convert_reduce_fusion.2
  9.1 0.2 convert_reduce_fusion.3
  9.2 0.1 copy.56
  9.3 0.1 copy.55
  9.5 0.1 copy.53
  9.6 0.5 convert_reduce_fusion
  10.7 1.2 select_reduce_fusion
  12.1 0.1 reshape.404
  12.2 0.1 copy.54
  12.3 0.1 reshape_squeeze.3
  12.5 0.1 stack.59.info_ref
  12.6 7.3 %shard_map.88 = bf16[112,2048]{1,0:T(8,128)(2,1)S(1)} custom-call(s32[5]{0:T(128)S(1)} %stack.59.info_ref, s32[7296]{0:T(1024)S(1)} %constant_dynamic-update-slice_fusion.17.lists_ref, bf16[2,224,2048]{2,1,0:T(8,128)(2,1)} %bitcast.138, bf16[2,2,96,128,128]{4,3,2,1,0:T(8,128)(2,1)} %bitcast.127), custom_call_target="tpu_custom_call" | custom-call | flops 4000000000 | tf_op jit(solution)/shard_map/pallas_call | solution.py:265
  19.9 5.2 %collective-permute-start.2 = (bf16[112,2048]{1,0:T(8,128)(2,1)S(1)}, bf16[112,2048]{1,0:T(8,128)(2,1)S(1)}, u32[]{:S(2)}, u32[]{:S(2)}) collective-permute-start(bf16[112,2048]{1,0:T(8,128)(2,1)S(1)} %shard_map.88), channel_id=1, source_target_pairs={{0,16},{24,8},{1,17},{25,9},{2,18},{26,10},{3,19},{27,11},{4,20},{... | collective-permute-start | bytes 1376264 | tf_op jit(solution)/shard_map/ppermute | solution.py:676
  25.1 7.3 %shard_map.86 = bf16[112,2048]{1,0:T(8,128)(2,1)S(1)} custom-call(s32[5]{0:T(128)S(1)} %stack.59.info_ref, s32[7296]{0:T(1024)S(1)} %constant_dynamic-update-slice_fusion.17.lists_ref, bf16[2,224,2048]{2,1,0:T(8,128)(2,1)} %bitcast.139, bf16[2,2,96,128,128]{4,3,2,1,0:T(8,128)(2,1)} %bitcast.128), custom_call_target="tpu_custom_call" | custom-call | flops 4000000000 | tf_op jit(solution)/shard_map/pallas_call | solution.py:265
  32.4 1.5 collective-permute-start
  33.9 0.9 collective-permute-done.2.rest_1_.rest_7_.rest_6_
  34.8 4.6 %copy-done = bf16[1,2,2,96,128,128]{5,4,3,2,1,0:T(8,128)(2,1)S(1)} copy-done((bf16[1,2,2,96,128,128]{5,4,3,2,1,0:T(8,128)(2,1)S(1)}, bf16[1,2,2,96,128,128]{5,4,3,2,1,0:T(8,128)(2,1)}, u32[]{:S(2)}) %copy-start) | copy-done | bytes 12582936
  39.4 11.7 %shard_map.89 = (bf16[112,2048]{1,0:T(8,128)(2,1)S(1)}, bf16[112,2048]{1,0:T(8,128)(2,1)S(1)}, bf16[2,64,112,128]{3,2,1,0:T(8,128)(2,1)}) custom-call(s32[5]{0:T(128)S(1)} %stack.59.info_ref, s32[7296]{0:T(1024)S(1)} %constant_dynamic-update-slice_fusion.17.lists_ref, bf16[2,2,96,128,128]{4,3,2,1,0:T(8,128)(2,1)S(1)} %bitcast.131, ...), custom_call_target="tpu_custom_call" | custom-call | flops 8000000000 | tf_op jit(solution)/shard_map/pallas_call | solution.py:265
  51.1 1.3 collective-permute-start.3
  52.4 11.9 %shard_map.87 = (bf16[112,2048]{1,0:T(8,128)(2,1)S(1)}, bf16[112,2048]{1,0:T(8,128)(2,1)S(1)}, bf16[2,64,112,128]{3,2,1,0:T(8,128)(2,1)}) custom-call(s32[5]{0:T(128)S(1)} %stack.59.info_ref, s32[7296]{0:T(1024)S(1)} %constant_dynamic-update-slice_fusion.17.lists_ref, bf16[2,2,96,128,128]{4,3,2,1,0:T(8,128)(2,1)S(1)} %bitcast.132, ...), custom_call_target="tpu_custom_call" | custom-call | flops 8000000000 | tf_op jit(solution)/shard_map/pallas_call | solution.py:265
  64.4 1.3 collective-permute-start.1
  65.7 11.5 %shard_map.92 = (bf16[112,2048]{1,0:T(8,128)(2,1)S(1)}, bf16[112,2048]{1,0:T(8,128)(2,1)S(1)}) custom-call(s32[5]{0:T(128)S(1)} %stack.59.info_ref, s32[7296]{0:T(1024)S(1)} %constant_dynamic-update-slice_fusion.17.lists_ref, bf16[2,2,96,128,128]{4,3,2,1,0:T(8,128)(2,1)S(1)} %bitcast.133, bf16[112,2048]{1,0:T(8,128)(2,1)S(1)} %collective-permute-done.3.rest_5_.rest_1_, ...), custom_call_target="tpu_custom_call" | custom-call | flops 12000000000 | tf_op jit(solution)/shard_map/pallas_call | solution.py:265
  77.2 5.1 %collective-permute-start.7 = (bf16[112,2048]{1,0:T(8,128)(2,1)S(1)}, bf16[112,2048]{1,0:T(8,128)(2,1)S(1)}, u32[]{:S(2)}, u32[]{:S(2)}) collective-permute-start(bf16[112,2048]{1,0:T(8,128)(2,1)S(1)} %get-tuple-element.31), channel_id=1, source_target_pairs={{0,16},{24,8},{1,17},{25,9},{2,18},{26,10},{3,19},{27,11},{4,20},{... | collective-permute-start | bytes 1376264 | tf_op jit(solution)/shard_map/ppermute | solution.py:676
  82.3 0.1 select_select_fusion
  82.4 3.4 %collective-permute-start.4 = (bf16[112,2048]{1,0:T(8,128)(2,1)S(1)}, bf16[112,2048]{1,0:T(8,128)(2,1)S(1)}, u32[]{:S(2)}, u32[]{:S(2)}) collective-permute-start(bf16[112,2048]{1,0:T(8,128)(2,1)S(1)} %select_select_fusion), channel_id=1, source_target_pairs={{0,24},{8,16},{16,8},{1,25},{9,17},{17,9},{2,26},{10,18},{18,10},{... | collective-permute-start | bytes 1376264 | tf_op jit(solution)/shard_map/ppermute | solution.py:691
  85.8 11.5 %shard_map.90 = (bf16[112,2048]{1,0:T(8,128)(2,1)S(1)}, bf16[112,2048]{1,0:T(8,128)(2,1)S(1)}) custom-call(s32[5]{0:T(128)S(1)} %stack.59.info_ref, s32[7296]{0:T(1024)S(1)} %constant_dynamic-update-slice_fusion.17.lists_ref, bf16[2,2,96,128,128]{4,3,2,1,0:T(8,128)(2,1)S(1)} %bitcast.134, bf16[112,2048]{1,0:T(8,128)(2,1)S(1)} %collective-permute-done.1.rest_1_, ...), custom_call_target="tpu_custom_call" | custom-call | flops 12000000000 | tf_op jit(solution)/shard_map/pallas_call | solution.py:265
  97.3 1.3 collective-permute-start.5
  98.6 2.4 collective-permute-done.7.rest_2_.rest_8_
  101.0 7.5 %shard_map.93 = (bf16[112,2048]{1,0:T(8,128)(2,1)S(1)}, bf16[112,2048]{1,0:T(8,128)(2,1)S(1)}) custom-call(s32[5]{0:T(128)S(1)} %stack.59.info_ref, s32[7296]{0:T(1024)S(1)} %constant_dynamic-update-slice_fusion.17.lists_ref, bf16[2,2,96,128,128]{4,3,2,1,0:T(8,128)(2,1)S(1)} %bitcast.135, bf16[112,2048]{1,0:T(8,128)(2,1)S(1)} %get-tuple-element.26.rest_6_.rest_1_.rest_7_, ...), custom_call_target="tpu_custom_call" | custom-call | flops 8000000000 | tf_op jit(solution)/shard_map/pallas_call | solution.py:265
  108.6 3.4 %collective-permute-start.13 = (bf16[112,2048]{1,0:T(8,128)(2,1)S(1)}, bf16[112,2048]{1,0:T(8,128)(2,1)S(1)}, u32[]{:S(2)}, u32[]{:S(2)}) collective-permute-start(bf16[112,2048]{1,0:T(8,128)(2,1)S(1)} %get-tuple-element.39), channel_id=1, source_target_pairs={{0,24},{8,16},{16,8},{1,25},{9,17},{17,9},{2,26},{10,18},{18,10},{... | collective-permute-start | bytes 1376264 | tf_op jit(solution)/shard_map/ppermute | solution.py:691
  111.9 12.6 %shard_map.91 = (bf16[112,2048]{1,0:T(8,128)(2,1)S(1)}, bf16[112,2048]{1,0:T(8,128)(2,1)S(1)}, bf16[112,2048]{1,0:T(8,128)(2,1)S(1)}, bf16[112,2048]{1,0:T(8,128)(2,1)S(1)}) custom-call(s32[5]{0:T(128)S(1)} %stack.59.info_ref, s32[7296]{0:T(1024)S(1)} %constant_dynamic-update-slice_fusion.17.lists_ref, bf16[2,2,96,128,128]{4,3,2,1,0:T(8,128)(2,1)S(1)} %bitcast.136, ...), custom_call_target="tpu_custom_call" | custom-call | flops 16000000000 | tf_op jit(solution)/shard_map/pallas_call | solution.py:265
  124.6 1.3 collective-permute-start.6
  125.9 7.5 %shard_map.94.rest_12_ = bf16[112,2048]{1,0:T(8,128)(2,1)S(1)} custom-call(s32[5]{0:T(128)S(1)} %stack.59.info_ref, s32[7296]{0:T(1024)S(1)} %constant_dynamic-update-slice_fusion.17.lists_ref, bf16[2,2,96,128,128]{4,3,2,1,0:T(8,128)(2,1)S(1)} %bitcast.137, bf16[112,2048]{1,0:T(8,128)(2,1)S(1)} %collective-permute-done.2.rest_1_.rest_7_.rest_6_, ...), custom_call_target="tpu_custom_call" | custom-call | flops 8000000000 | tf_op jit(solution)/shard_map/pallas_call | solution.py:265
  133.4 1.3 collective-permute-start.12
  134.7 1.3 collective-permute-start.9
  136.0 1.3 collective-permute-start.10
  137.3 1.5 collective-permute-start.8
  138.8 1.3 collective-permute-start.11
  140.2 18.6 %shard_map.95 = (bf16[64,448,128]{2,1,0:T(8,128)(2,1)S(1)}, bf16[64,448,128]{2,1,0:T(8,128)(2,1)}, bf16[17,448,128]{2,1,0:T(8,128)(2,1)}) custom-call(s32[5]{0:T(128)S(1)} %stack.59.info_ref, s32[7296]{0:T(1024)S(1)} %constant_dynamic-update-slice_fusion.17.lists_ref, bf16[2,224,2048]{2,1,0:T(8,128)(2,1)} %bitcast.140, ...), custom_call_target="tpu_custom_call" | custom-call | flops 16000000000 | tf_op jit(solution)/shard_map/pallas_call | solution.py:265
  158.8 2.1 collective-permute-done.8.rest_1_
  160.9 10.2 %shard_map.96 = (bf16[8,96,16,128]{3,2,1,0:T(8,128)(2,1)}, bf16[17,448,128]{2,1,0:T(8,128)(2,1)}) custom-call(s32[5]{0:T(128)S(1)} %stack.59.info_ref, s32[7296]{0:T(1024)S(1)} %constant_dynamic-update-slice_fusion.17.lists_ref, bf16[64,448,128]{2,1,0:T(8,128)(2,1)S(1)} %get-tuple-element.35.rest_0_, bf16[112,2048]{1,0:T(8,128)(2,1)S(1)} %collective-permute-done.8.rest_1_, ...), custom_call_target="tpu_custom_call" | custom-call | flops 8000000000 | tf_op jit(solution)/shard_map/pallas_call | solution.py:265
  171.1 25.4 %shard_map.97 = bf16[8,96,16,128]{3,2,1,0:T(8,128)(2,1)} custom-call(s32[5]{0:T(128)S(1)} %stack.59.info_ref, s32[7296]{0:T(1024)S(1)} %constant_dynamic-update-slice_fusion.17.lists_ref, bf16[17,448,128]{2,1,0:T(8,128)(2,1)} %get-tuple-element.41.rest_0_, bf16[17,448,128]{2,1,0:T(8,128)(2,1)} %get-tuple-element.42.rest_1_, ...), custom_call_target="tpu_custom_call" | custom-call | flops 16000000000 | tf_op jit(solution)/shard_map/pallas_call | solution.py:265
  196.6 22.8 %reduce-scatter.3.cloned.1.call-done = bf16[1,96,16,128]{3,2,1,0:T(8,128)(2,1)} async-done(((bf16[8,96,16,128]{3,2,1,0:T(8,128)(2,1)}), bf16[1,96,16,128]{3,2,1,0:T(8,128)(2,1)}) %reduce-scatter.3.cloned.1.call-update) | async-done | bytes 393232 | tf_op jit(solution)/shard_map/reduce_scatter | solution.py:811
  219.4 42.0 %reduce-scatter.5.cloned.1.call-done = bf16[1,96,16,128]{3,2,1,0:T(8,128)(2,1)} async-done(((bf16[8,96,16,128]{3,2,1,0:T(8,128)(2,1)}), bf16[1,96,16,128]{3,2,1,0:T(8,128)(2,1)}) %reduce-scatter.5.cloned.1.call-update) | async-done | bytes 393232 | tf_op jit(solution)/shard_map/reduce_scatter | solution.py:811
  261.4 1.2 maximum_convert_fusion
  262.6 4.3 %fusion.2 = (f32[1,2,96,16,128]{4,3,2,1,0:T(8,128)}, f32[2,96,16,128]{3,2,1,0:T(8,128)}) fusion(f32[1,2,96,16,128]{4,3,2,1,0:T(8,128)S(1)} %copy-done.1, f32[1,2,96,16,128]{4,3,2,1,0:T(8,128)S(1)} %copy-done.2, f32[2,96,16,128]{3,2,1,0:T(8,128)S(1)} %maximum_convert_fusion, f32[1,2,96,16,128]{4,3,2,1,0:T(8,128)} %param.12), kind=kLoop, calls=%fused_computation.6 | loop fusion | flops 6291456 | bytes 9437184 | tf_op jit(solution)/shard_map/broadcast_in_dim | solution.py:819
  (51 shorter events, 1.1 us)
Async XLA Ops:
  7.2 212.2 %reduce-scatter.3.cloned.1.call-start = ((), (), s32[]{:S(2)}) async-start(), calls=%async_computation.2 | async-start | bytes 3538944 | tf_op jit(solution)/shard_map/reduce_scatter | solution.py:811
  19.9 14.9 %collective-permute-start.2 = (bf16[112,2048]{1,0:T(8,128)(2,1)S(1)}, bf16[112,2048]{1,0:T(8,128)(2,1)S(1)}, u32[]{:S(2)}, u32[]{:S(2)}) collective-permute-start(bf16[112,2048]{1,0:T(8,128)(2,1)S(1)} %shard_map.88), channel_id=1, source_target_pairs={{0,16},{24,8},{1,17},{25,9},{2,18},{26,10},{3,19},{27,11},{4,20},{... | collective-permute-start | bytes 1376264 | tf_op jit(solution)/shard_map/ppermute | solution.py:676
  32.4 20.0 %collective-permute-start = (bf16[112,2048]{1,0:T(8,128)(2,1)S(1)}, bf16[112,2048]{1,0:T(8,128)(2,1)S(1)}, u32[]{:S(2)}, u32[]{:S(2)}) collective-permute-start(bf16[112,2048]{1,0:T(8,128)(2,1)S(1)} %shard_map.86), channel_id=1, source_target_pairs={{0,8},{24,16},{1,9},{25,17},{2,10},{26,18},{3,11},{27,19},{4,12},{... | collective-permute-start | bytes 1376264 | tf_op jit(solution)/shard_map/ppermute | solution.py:676
  34.8 4.6 %copy-start = (bf16[1,2,2,96,128,128]{5,4,3,2,1,0:T(8,128)(2,1)S(1)}, bf16[1,2,2,96,128,128]{5,4,3,2,1,0:T(8,128)(2,1)}, u32[]{:S(2)}) copy-start(bf16[1,2,2,96,128,128]{5,4,3,2,1,0:T(8,128)(2,1)} %param.9) | copy-start | bytes 37748740
  51.1 14.5 %collective-permute-start.3 = (bf16[112,2048]{1,0:T(8,128)(2,1)S(1)}, bf16[112,2048]{1,0:T(8,128)(2,1)S(1)}, u32[]{:S(2)}, u32[]{:S(2)}) collective-permute-start(bf16[112,2048]{1,0:T(8,128)(2,1)S(1)} %get-tuple-element.25), channel_id=1, source_target_pairs={{16,0},{8,24},{17,1},{9,25},{18,2},{10,26},{19,3},{11,27},{20,4},{... | collective-permute-start | bytes 1376264 | tf_op jit(solution)/shard_map/ppermute | solution.py:679
  64.4 17.9 %collective-permute-start.1 = (bf16[112,2048]{1,0:T(8,128)(2,1)S(1)}, bf16[112,2048]{1,0:T(8,128)(2,1)S(1)}, u32[]{:S(2)}, u32[]{:S(2)}) collective-permute-start(bf16[112,2048]{1,0:T(8,128)(2,1)S(1)} %get-tuple-element.23), channel_id=1, source_target_pairs={{8,0},{16,24},{9,1},{17,25},{10,2},{18,26},{11,3},{19,27},{12,4},{... | collective-permute-start | bytes 1376264 | tf_op jit(solution)/shard_map/ppermute | solution.py:679
  77.2 23.8 %collective-permute-start.7 = (bf16[112,2048]{1,0:T(8,128)(2,1)S(1)}, bf16[112,2048]{1,0:T(8,128)(2,1)S(1)}, u32[]{:S(2)}, u32[]{:S(2)}) collective-permute-start(bf16[112,2048]{1,0:T(8,128)(2,1)S(1)} %get-tuple-element.31), channel_id=1, source_target_pairs={{0,16},{24,8},{1,17},{25,9},{2,18},{26,10},{3,19},{27,11},{4,20},{... | collective-permute-start | bytes 1376264 | tf_op jit(solution)/shard_map/ppermute | solution.py:676
  82.4 53.6 %collective-permute-start.4 = (bf16[112,2048]{1,0:T(8,128)(2,1)S(1)}, bf16[112,2048]{1,0:T(8,128)(2,1)S(1)}, u32[]{:S(2)}, u32[]{:S(2)}) collective-permute-start(bf16[112,2048]{1,0:T(8,128)(2,1)S(1)} %select_select_fusion), channel_id=1, source_target_pairs={{0,24},{8,16},{16,8},{1,25},{9,17},{17,9},{2,26},{10,18},{18,10},{... | collective-permute-start | bytes 1376264 | tf_op jit(solution)/shard_map/ppermute | solution.py:691
  97.3 14.6 %collective-permute-start.5 = (bf16[112,2048]{1,0:T(8,128)(2,1)S(1)}, bf16[112,2048]{1,0:T(8,128)(2,1)S(1)}, u32[]{:S(2)}, u32[]{:S(2)}) collective-permute-start(bf16[112,2048]{1,0:T(8,128)(2,1)S(1)} %get-tuple-element.27), channel_id=1, source_target_pairs={{0,8},{24,16},{1,9},{25,17},{2,10},{26,18},{3,11},{27,19},{4,12},{... | collective-permute-start | bytes 1376264 | tf_op jit(solution)/shard_map/ppermute | solution.py:676
  108.6 28.7 %collective-permute-start.13 = (bf16[112,2048]{1,0:T(8,128)(2,1)S(1)}, bf16[112,2048]{1,0:T(8,128)(2,1)S(1)}, u32[]{:S(2)}, u32[]{:S(2)}) collective-permute-start(bf16[112,2048]{1,0:T(8,128)(2,1)S(1)} %get-tuple-element.39), channel_id=1, source_target_pairs={{0,24},{8,16},{16,8},{1,25},{9,17},{17,9},{2,26},{10,18},{18,10},{... | collective-permute-start | bytes 1376264 | tf_op jit(solution)/shard_map/ppermute | solution.py:691
  124.6 14.3 %collective-permute-start.6 = (bf16[112,2048]{1,0:T(8,128)(2,1)S(1)}, bf16[112,2048]{1,0:T(8,128)(2,1)S(1)}, u32[]{:S(2)}, u32[]{:S(2)}) collective-permute-start(bf16[112,2048]{1,0:T(8,128)(2,1)S(1)} %get-tuple-element.30), channel_id=1, source_target_pairs={{0,24},{8,16},{16,8},{1,25},{9,17},{17,9},{2,26},{10,18},{18,10},{... | collective-permute-start | bytes 1376264 | tf_op jit(solution)/shard_map/ppermute | solution.py:691
  133.4 25.4 %collective-permute-start.12 = (bf16[112,2048]{1,0:T(8,128)(2,1)S(1)}, bf16[112,2048]{1,0:T(8,128)(2,1)S(1)}, u32[]{:S(2)}, u32[]{:S(2)}) collective-permute-start(bf16[112,2048]{1,0:T(8,128)(2,1)S(1)} %shard_map.94.rest_12_), channel_id=1, source_target_pairs={{8,0},{9,1},{10,2},{11,3},{12,4},{13,5},{14,6},{15,7}} | collective-permute-start | bytes 1376264 | tf_op jit(solution)/shard_map/ppermute | solution.py:766
  134.7 24.1 %collective-permute-start.9 = (bf16[112,2048]{1,0:T(8,128)(2,1)S(1)}, bf16[112,2048]{1,0:T(8,128)(2,1)S(1)}, u32[]{:S(2)}, u32[]{:S(2)}) collective-permute-start(bf16[112,2048]{1,0:T(8,128)(2,1)S(1)} %shard_map.94.rest_12_), channel_id=1, source_target_pairs={{16,0},{17,1},{18,2},{19,3},{20,4},{21,5},{22,6},{23,7}} | collective-permute-start | bytes 1376264 | tf_op jit(solution)/shard_map/ppermute | solution.py:767
  136.0 22.8 %collective-permute-start.10 = (bf16[112,2048]{1,0:T(8,128)(2,1)S(1)}, bf16[112,2048]{1,0:T(8,128)(2,1)S(1)}, u32[]{:S(2)}, u32[]{:S(2)}) collective-permute-start(bf16[112,2048]{1,0:T(8,128)(2,1)S(1)} %get-tuple-element.36), channel_id=1, source_target_pairs={{16,0},{17,1},{18,2},{19,3},{20,4},{21,5},{22,6},{23,7}} | collective-permute-start | bytes 1376264 | tf_op jit(solution)/shard_map/ppermute | solution.py:767
  137.3 23.6 %collective-permute-start.8 = (bf16[112,2048]{1,0:T(8,128)(2,1)S(1)}, bf16[112,2048]{1,0:T(8,128)(2,1)S(1)}, u32[]{:S(2)}, u32[]{:S(2)}) collective-permute-start(bf16[112,2048]{1,0:T(8,128)(2,1)S(1)} %get-tuple-element.36), channel_id=1, source_target_pairs={{8,0},{9,1},{10,2},{11,3},{12,4},{13,5},{14,6},{15,7}} | collective-permute-start | bytes 1376264 | tf_op jit(solution)/shard_map/ppermute | solution.py:766
  138.8 19.9 %collective-permute-start.11 = (bf16[112,2048]{1,0:T(8,128)(2,1)S(1)}, bf16[112,2048]{1,0:T(8,128)(2,1)S(1)}, u32[]{:S(2)}, u32[]{:S(2)}) collective-permute-start(bf16[112,2048]{1,0:T(8,128)(2,1)S(1)} %get-tuple-element.38), channel_id=1, source_target_pairs={{0,24},{8,16},{16,8},{1,25},{9,17},{17,9},{2,26},{10,18},{18,10},{... | collective-permute-start | bytes 1376264 | tf_op jit(solution)/shard_map/ppermute | solution.py:691
  171.1 90.3 %reduce-scatter.5.cloned.1.call-start = ((), (), s32[]{:S(2)}) async-start(), calls=%async_computation.3 | async-start | bytes 3538944 | tf_op jit(solution)/shard_map/reduce_scatter | solution.py:811
  196.5 66.1 %copy-start.2 = (f32[1,2,96,16,128]{4,3,2,1,0:T(8,128)S(1)}, f32[1,2,96,16,128]{4,3,2,1,0:T(8,128)}, u32[]{:S(2)}) copy-start(f32[1,2,96,16,128]{4,3,2,1,0:T(8,128)} %param.13) | copy-start | bytes 4718596
  196.6 66.0 %copy-start.1 = (f32[1,2,96,16,128]{4,3,2,1,0:T(8,128)S(1)}, f32[1,2,96,16,128]{4,3,2,1,0:T(8,128)}, u32[]{:S(2)}) copy-start(f32[1,2,96,16,128]{4,3,2,1,0:T(8,128)} %param.11) | copy-start | bytes 4718596
Sparse Core Ops, SparseCore 0:
  171.2 48.1 reduce-scatter.2
  221.7 39.6 reduce-scatter.4

commit v2 on v1

--- a/solution.py
+++ b/solution.py
@@ -24,6 +24,7 @@
 OWN_VMEM = 40 * 1024 * 1024
 COST = 4_000_000_000
 LOCAL = None
+WINDOW = "window"
 ENTER_COST = 1
 LOW_LAYER, HIGH_LAYER, OWN_LAYER, HIGH, GROUP = range(5)
 UP_WIDE, DOWN_WIDE, DOWN_NARROW, UP_NARROW = range(4)
@@ -243,6 +244,10 @@
             self.up, self.down = local.at[0], local.at[1]
 
 
+def space_of(space):
+    return pltpu.HBM if space is WINDOW else space
+
+
 def stage(kernel, local_in, remote_in, outs, scratch, operands, cost, vmem=CHAIN_VMEM):
     info, lists, weights = operands
     held = [] if weights is None else [pltpu.with_memory_space_constraint(weights, pltpu.VMEM)]
@@ -269,7 +274,8 @@
         + [any_spec] * len(remote_in),
         out_specs=[any_spec if space is pltpu.HBM else vmem_spec for space, _ in outs],
         out_shape=[
-            shape if space is LOCAL else space(shape.shape, shape.dtype) for space, shape in outs
+            shape if space is LOCAL else space_of(space)(shape.shape, shape.dtype)
+            for space, shape in outs
         ],
         scratch_shapes=scratch,
         cost_estimate=pl.CostEstimate(flops=cost, transcendentals=0, bytes_accessed=0),
@@ -359,7 +365,7 @@
     return stage(kernel, [], [tokens, unloaded], outs, scratch, operands, COST * ENTER_COST, CHAIN_VMEM)
 
 
-def turn_call(x, targets, h, operands):
+def turn_call(x, targets, h, operands, entries=()):
     rows, width = x.shape
 
     def kernel(layer, info, ins, results, scratch):
@@ -377,9 +383,13 @@
             difference = residue[:, cols].astype(jnp.float32) - aim[:, cols].astype(jnp.float32)
             residue[:, cols] = difference.astype(jnp.bfloat16)
         backward_rows(x_ref, residue, out, own, layer_refs, slopes)
+        if entries:
+            high, group = info[HIGH] == 1, info[GROUP]
+            conditions = [~high & (group == 0), ~high & (group != 0), high]
+            pick_rows(results[2], list(zip(conditions, ins[:3])))
 
     return stage(
-        kernel, [x], [targets], [(LOCAL, shape_of(x.shape))] * 2,
+        kernel, [x] + list(entries), [targets], [(LOCAL, shape_of(x.shape))] * (2 + bool(entries)),
         layer_scratch(rows, width) + slope_scratch(rows)
         + [pltpu.VMEM((rows, width), jnp.bfloat16), pltpu.SemaphoreType.DMA],
         operands, 3 * COST
@@ -394,10 +404,10 @@
             target[...] = source[...]
 
 
-def backward_call(xs, saved, cot, whichs, operands, turned=None, last=None, entries=()):
+def backward_call(xs, saved, cot, whichs, operands, turned=None, last=None):
     rows, width = cot.shape
     steps = len(whichs)
-    local = list(xs) + [cot] + ([] if turned is None else [turned]) + list(entries)
+    local = list(xs) + [cot] + ([] if turned is None else [turned])
 
     def kernel(layer, info, ins, results, scratch):
         *layer_refs, slopes, sem = scratch
@@ -424,15 +434,12 @@
                     (~high & (group != last), ins[steps + 1]),
                 ],
             )
-        if entries:
-            conditions = [~high & (group != last), ~high & (group == last), high]
-            pick_rows(results[steps + 1], list(zip(conditions, ins[steps + 2 :])))
 
     scratch = [
         pltpu.VMEM((steps, FF_BLOCKS, rows, BS), jnp.bfloat16),
         pltpu.SemaphoreType.DMA((steps,)),
     ]
-    outs = [(LOCAL, shape_of(cot.shape))] * (steps + (turned is not None) + bool(entries))
+    outs = [(LOCAL, shape_of(cot.shape))] * (steps + (turned is not None))
     return stage(
         kernel, local, [array for array, _ in saved], outs, layer_scratch(rows, width) + scratch,
         operands, 2 * COST * steps
@@ -564,7 +571,7 @@
     return stage(
         kernel, [hidden], refs,
         [
-            (LOCAL, shape_of((shares, total, BS // shares, BS))),
+            (WINDOW, shape_of((shares, total, BS // shares, BS))),
             (pltpu.HBM, shape_of((width // BS + 1, all_rows, BS))),
         ],
         [
@@ -624,7 +631,7 @@
 
     return stage(
         kernel, [], [normed, split, slopes, unloaded],
-        [(LOCAL, shape_of((shares, total, BS // shares, BS)))],
+        [(WINDOW, shape_of((shares, total, BS // shares, BS)))],
         [
             pltpu.VMEM((FF_BLOCKS, part_rows, BS), jnp.float32),
             pltpu.VMEM((FF_BLOCKS, all_rows, BS), jnp.bfloat16),
@@ -647,6 +654,30 @@
     spread = jnp.sqrt(variance_next / (1.0 - beta_second**update_count))
     step_direction = corrected / (spread + adam_eps)
     return (step_direction, master - learn_rate * (step_direction + decay_rate * master))
+
+
+def adam_call(share, part, state, token_total, filled=()):
+    shape = state[0].shape
+    span = pl.BlockSpec((None,) + shape[1:], lambda i: (part, 0, 0, 0))
+    whole = pl.BlockSpec(share.shape, lambda i: (0, 0, 0))
+
+    def kernel(share_ref, master_ref, moment_ref, variance_ref, *rest):
+        direction, master_next = rest[-2:]
+        direction[...], master_next[...] = adam_update(
+            share_ref[...].astype(jnp.float32), master_ref[...], moment_ref[...], variance_ref[...],
+            token_total
+        )
+
+    return pl.pallas_call(
+        kernel,
+        grid=(1,),
+        in_specs=[whole] + [span] * 3 + [pl.BlockSpec(memory_space=pl.ANY)] * len(filled),
+        out_specs=[span, span],
+        out_shape=[shape_of(shape, jnp.float32)] * 2,
+        input_output_aliases={4 + i: i for i in range(len(filled))},
+        name="adam",
+        compiler_params=pltpu.CompilerParams(vmem_limit_bytes=CHAIN_VMEM),
+    )(share, *state, *filled)
 
 
 def shards(tokens, targets, weights, pattern, master, moment, variance):
@@ -718,7 +749,9 @@
     mirrored = groups == 2
     turned = []
     for h in halves:
-        turned.append(turn_call(current[h], targets, h, operands))
+        entries = [x_high[1][1], x_low[1][1]] if mirrored and h else []
+        turned.append(turn_call(current[h], targets, h, operands, entries))
+    x_sent = turned[1][2] if mirrored else None
     cot_high[0] = [t[0] for t in turned]
     current = [t[1] for t in turned]
     for i in range(groups - 1):
@@ -739,13 +772,11 @@
         tops, bottoms = slope_high[last][h], slope_low[last][h]
         sending = dict(turned=cot_high[0][h], last=last) if mirrored else {}
         if h == 0:
-            if mirrored:
-                sending["entries"] = [x_high[0][1], x_high[1][1], x_low[1][1]]
             moved = backward_call(
-                [top, bottom], [tops, bottoms], entering[h], [HIGH_LAYER, LOW_LAYER], operands, **sending
+                [top, bottom], [tops, bottoms], entering[h], [HIGH_LAYER, LOW_LAYER], operands,
+                **sending
             )
             cot_low[last][h], current[h], *sent = moved
-            x_sent = sent[1] if mirrored else None
         else:
             cot_low[last][h], *sent = backward_call(
                 [top], [tops], entering[h], [HIGH_LAYER], operands, **sending
@@ -808,14 +839,16 @@
     )
 
     def reduce(grads):
-        return lax.psum_scatter(grads, "dp", scatter_dimension=0, tiled=True)[0].astype(jnp.float32)
+        return lax.psum_scatter(grads, "dp", scatter_dimension=0, tiled=True)[0]
 
     down_share = reduce(downs)
-    up_share = reduce(up_grads_call(far(split), far(normed), far(slopes), width, shares, unloaded, (info, lists, None)))
+    up_share = reduce(
+        up_grads_call(far(split), far(normed), far(slopes), width, shares, unloaded, (info, lists, None))
+    )
     token_total = 2 * rows * shares
-    step_direction, master_next = adam_update(
-        jnp.stack([down_share, up_share])[::-1], master[0], moment[0], variance[0], token_total
-    )
+    state = (far(master[0]), far(moment[0]), far(variance[0]))
+    filled = adam_call(far(down_share), 1, state, token_total)
+    step_direction, master_next = adam_call(far(up_share), 0, state, token_total, filled)
     return (step_direction[None], master_next[None])
 
 

time: 274 us -> 278 us (1.015)
  Pallas kernels: 143 us -> 150 us
  other arithmetic: 8.65 us -> 3.08 us
    ppermute x4, waiting for transfers between devices: 3.29 us -> 10.6 us  [inward(): return lax.ppermute(x, 'section', lane(i, h))]
    pallas_call x0 -> x2, Pallas kernels: none -> 6.93 us  [adam_call(): pl.pallas_call(kernel, grid=(1,), in_specs=[whole] + [span] * 3 + [pl.Blo...]
    reduce_scatter x2, waiting for transfers between devices: 64.8 us -> 60.5 us  [reduce(): return lax.psum_scatter(grads, 'dp', scatter_dimension=0, tiled=True)[0]]
    broadcast_in_dim x1 -> x0, other arithmetic: 4.3 us -> none  [shards(): return (step_direction[None], master_next[None])]
  transfers between devices with their start and end apart: 16 -> 16, of which waited for: 5 -> 4; matrix products, arithmetic and copies ran while one was open for 0% -> 0% of each run, Pallas kernels for 46% -> 47%
where the time goes in v2:
time: 278 us; the launch traced here: 277 us
  Pallas kernels  150 us (54%)
  waiting for transfers between devices  71.1 us (26%)
  starting transfers between devices  31.4 us (11%)
  between operations  14.5 us (5%)
  local copies, waits for them, and re-layouts  6.83 us (2%)
  other arithmetic  3.08 us (1%)
    pallas_call x12, Pallas kernels, stage(): pl.pallas_call(body, in_specs=[smem_spec, smem_spec] + [vmem_spec] * (len...  144 us
    reduce_scatter x2, waiting for transfers between devices, reduce(): return lax.psum_scatter(grads, 'dp', scatter_dimension=0, tiled=True)[0]  60.5 us
    ppermute x4, starting transfers between devices, inward(): return lax.ppermute(x, 'section', lane(i, h))  13 us
    ppermute x4, waiting for transfers between devices, inward(): return lax.ppermute(x, 'section', lane(i, h))  10.6 us
    ppermute x4, starting transfers between devices, swap(): return lax.ppermute(sent, 'section', pairs)  10.3 us
    pallas_call x2, Pallas kernels, adam_call(): pl.pallas_call(kernel, grid=(1,), in_specs=[whole] + [span] * 3 + [pl.Blo...  6.93 us
  transfers between devices with their start and end apart: 16, of which 4 were waited for; matrix products, arithmetic and copies ran while one was open for 0% of the time, Pallas kernels for 47%

profile of v2, /device:TPU:0, one launch (start us, length us, event | category | flops | bytes accessed | tf_op | source)
XLA Modules:
  0.0 277.3 jit_solution(15645606172299848547)
XLA Ops:
  7.2 0.7 slice.20
  7.9 0.7 copy.60
  8.7 0.4 convert_reduce_fusion.2
  9.1 0.2 convert_reduce_fusion.3
  9.2 0.1 copy.58
  9.3 0.1 copy.57
  9.5 0.1 copy.55
  9.6 0.5 convert_reduce_fusion
  10.3 0.1 constant_dynamic-update-slice_fusion.4
  10.4 0.1 constant_dynamic-update-slice_fusion.2
  10.7 1.2 select_reduce_fusion
  12.1 0.1 reshape.400
  12.2 0.1 copy.56
  12.3 0.1 reshape_squeeze.3
  12.5 0.1 stack.51.info_ref
  12.6 7.3 %shard_map.88 = bf16[112,2048]{1,0:T(8,128)(2,1)S(1)} custom-call(s32[5]{0:T(128)S(1)} %stack.51.info_ref, s32[7296]{0:T(1024)S(1)} %constant_dynamic-update-slice_fusion.17.lists_ref, bf16[2,224,2048]{2,1,0:T(8,128)(2,1)} %bitcast.113, bf16[2,2,96,128,128]{4,3,2,1,0:T(8,128)(2,1)} %bitcast.102), custom_call_target="tpu_custom_call" | custom-call | flops 4000000000 | tf_op jit(solution)/shard_map/pallas_call | solution.py:270
  19.9 5.2 %collective-permute-start.2 = (bf16[112,2048]{1,0:T(8,128)(2,1)S(1)}, bf16[112,2048]{1,0:T(8,128)(2,1)S(1)}, u32[]{:S(2)}, u32[]{:S(2)}) collective-permute-start(bf16[112,2048]{1,0:T(8,128)(2,1)S(1)} %shard_map.88), channel_id=1, source_target_pairs={{0,16},{24,8},{1,17},{25,9},{2,18},{26,10},{3,19},{27,11},{4,20},{... | collective-permute-start | bytes 1376264 | tf_op jit(solution)/shard_map/ppermute | solution.py:707
  25.1 7.3 %shard_map.86 = bf16[112,2048]{1,0:T(8,128)(2,1)S(1)} custom-call(s32[5]{0:T(128)S(1)} %stack.51.info_ref, s32[7296]{0:T(1024)S(1)} %constant_dynamic-update-slice_fusion.17.lists_ref, bf16[2,224,2048]{2,1,0:T(8,128)(2,1)} %bitcast.114, bf16[2,2,96,128,128]{4,3,2,1,0:T(8,128)(2,1)} %bitcast.103), custom_call_target="tpu_custom_call" | custom-call | flops 4000000000 | tf_op jit(solution)/shard_map/pallas_call | solution.py:270
  32.4 1.5 collective-permute-start
  33.9 0.9 collective-permute-done.2.rest_1_.rest_3_.rest_6_
  34.8 4.6 %copy-done = bf16[1,2,2,96,128,128]{5,4,3,2,1,0:T(8,128)(2,1)S(1)} copy-done((bf16[1,2,2,96,128,128]{5,4,3,2,1,0:T(8,128)(2,1)S(1)}, bf16[1,2,2,96,128,128]{5,4,3,2,1,0:T(8,128)(2,1)}, u32[]{:S(2)}) %copy-start) | copy-done | bytes 12582936
  39.4 11.8 %shard_map.89 = (bf16[112,2048]{1,0:T(8,128)(2,1)S(1)}, bf16[112,2048]{1,0:T(8,128)(2,1)S(1)}, bf16[2,64,112,128]{3,2,1,0:T(8,128)(2,1)}) custom-call(s32[5]{0:T(128)S(1)} %stack.51.info_ref, s32[7296]{0:T(1024)S(1)} %constant_dynamic-update-slice_fusion.17.lists_ref, bf16[2,2,96,128,128]{4,3,2,1,0:T(8,128)(2,1)S(1)} %bitcast.106, ...), custom_call_target="tpu_custom_call" | custom-call | flops 8000000000 | tf_op jit(solution)/shard_map/pallas_call | solution.py:270
  51.2 1.3 collective-permute-start.3
  52.5 12.0 %shard_map.87 = (bf16[112,2048]{1,0:T(8,128)(2,1)S(1)}, bf16[112,2048]{1,0:T(8,128)(2,1)S(1)}, bf16[2,64,112,128]{3,2,1,0:T(8,128)(2,1)}) custom-call(s32[5]{0:T(128)S(1)} %stack.51.info_ref, s32[7296]{0:T(1024)S(1)} %constant_dynamic-update-slice_fusion.17.lists_ref, bf16[2,2,96,128,128]{4,3,2,1,0:T(8,128)(2,1)S(1)} %bitcast.107, ...), custom_call_target="tpu_custom_call" | custom-call | flops 8000000000 | tf_op jit(solution)/shard_map/pallas_call | solution.py:270
  64.5 1.3 collective-permute-start.1
  65.8 11.6 %shard_map.90 = (bf16[112,2048]{1,0:T(8,128)(2,1)S(1)}, bf16[112,2048]{1,0:T(8,128)(2,1)S(1)}, bf16[112,2048]{1,0:T(8,128)(2,1)S(1)}) custom-call(s32[5]{0:T(128)S(1)} %stack.51.info_ref, s32[7296]{0:T(1024)S(1)} %constant_dynamic-update-slice_fusion.17.lists_ref, bf16[2,2,96,128,128]{4,3,2,1,0:T(8,128)(2,1)S(1)} %bitcast.108, ...), custom_call_target="tpu_custom_call" | custom-call | flops 12000000000 | tf_op jit(solution)/shard_map/pallas_call | solution.py:270
  77.4 3.4 %collective-permute-start.5 = (bf16[112,2048]{1,0:T(8,128)(2,1)S(1)}, bf16[112,2048]{1,0:T(8,128)(2,1)S(1)}, u32[]{:S(2)}, u32[]{:S(2)}) collective-permute-start(bf16[112,2048]{1,0:T(8,128)(2,1)S(1)} %get-tuple-element.31), channel_id=1, source_target_pairs={{0,24},{8,16},{16,8},{1,25},{9,17},{17,9},{2,26},{10,18},{18,10},{... | collective-permute-start | bytes 1376264 | tf_op jit(solution)/shard_map/ppermute | solution.py:722
  80.7 5.1 %collective-permute-start.6 = (bf16[112,2048]{1,0:T(8,128)(2,1)S(1)}, bf16[112,2048]{1,0:T(8,128)(2,1)S(1)}, u32[]{:S(2)}, u32[]{:S(2)}) collective-permute-start(bf16[112,2048]{1,0:T(8,128)(2,1)S(1)} %get-tuple-element.32), channel_id=1, source_target_pairs={{0,16},{24,8},{1,17},{25,9},{2,18},{26,10},{3,19},{27,11},{4,20},{... | collective-permute-start | bytes 1376264 | tf_op jit(solution)/shard_map/ppermute | solution.py:707
  85.9 3.4 %collective-permute-start.4 = (bf16[112,2048]{1,0:T(8,128)(2,1)S(1)}, bf16[112,2048]{1,0:T(8,128)(2,1)S(1)}, u32[]{:S(2)}, u32[]{:S(2)}) collective-permute-start(bf16[112,2048]{1,0:T(8,128)(2,1)S(1)} %select_select_fusion), channel_id=1, source_target_pairs={{0,24},{8,16},{16,8},{1,25},{9,17},{17,9},{2,26},{10,18},{18,10},{... | collective-permute-start | bytes 1376264 | tf_op jit(solution)/shard_map/ppermute | solution.py:722
  89.3 11.6 %shard_map.94 = (bf16[112,2048]{1,0:T(8,128)(2,1)S(1)}, bf16[112,2048]{1,0:T(8,128)(2,1)S(1)}) custom-call(s32[5]{0:T(128)S(1)} %stack.51.info_ref, s32[7296]{0:T(1024)S(1)} %constant_dynamic-update-slice_fusion.17.lists_ref, bf16[2,2,96,128,128]{4,3,2,1,0:T(8,128)(2,1)S(1)} %bitcast.109, bf16[112,2048]{1,0:T(8,128)(2,1)S(1)} %collective-permute-done.1.rest_1_, ...), custom_call_target="tpu_custom_call" | custom-call | flops 12000000000 | tf_op jit(solution)/shard_map/pallas_call | solution.py:270
  100.9 1.3 collective-permute-start.7
  102.2 9.7 %collective-permute-done.6.rest_2_.rest_8_ = bf16[112,2048]{1,0:T(8,128)(2,1)S(1)} collective-permute-done((bf16[112,2048]{1,0:T(8,128)(2,1)S(1)}, bf16[112,2048]{1,0:T(8,128)(2,1)S(1)}, u32[]{:S(2)}, u32[]{:S(2)}) %collective-permute-start.6) | collective-permute-done | bytes 458784 | tf_op jit(solution)/shard_map/ppermute | solution.py:707
  111.9 7.5 %shard_map.91 = (bf16[112,2048]{1,0:T(8,128)(2,1)S(1)}, bf16[112,2048]{1,0:T(8,128)(2,1)S(1)}) custom-call(s32[5]{0:T(128)S(1)} %stack.51.info_ref, s32[7296]{0:T(1024)S(1)} %constant_dynamic-update-slice_fusion.17.lists_ref, bf16[2,2,96,128,128]{4,3,2,1,0:T(8,128)(2,1)S(1)} %bitcast.110, bf16[112,2048]{1,0:T(8,128)(2,1)S(1)} %get-tuple-element.30.rest_2_.rest_1_.rest_7_, ...), custom_call_target="tpu_custom_call" | custom-call | flops 8000000000 | tf_op jit(solution)/shard_map/pallas_call | solution.py:270
  119.5 7.5 %shard_map.92.rest_12_ = bf16[112,2048]{1,0:T(8,128)(2,1)S(1)} custom-call(s32[5]{0:T(128)S(1)} %stack.51.info_ref, s32[7296]{0:T(1024)S(1)} %constant_dynamic-update-slice_fusion.17.lists_ref, bf16[2,2,96,128,128]{4,3,2,1,0:T(8,128)(2,1)S(1)} %bitcast.111, bf16[112,2048]{1,0:T(8,128)(2,1)S(1)} %collective-permute-done.2.rest_1_.rest_3_.rest_6_, ...), custom_call_target="tpu_custom_call" | custom-call | flops 8000000000 | tf_op jit(solution)/shard_map/pallas_call | solution.py:270
  127.0 1.3 collective-permute-start.12
  128.3 1.3 collective-permute-start.9
  129.6 2.2 collective-permute-start.13
  131.8 12.6 %shard_map.95 = (bf16[112,2048]{1,0:T(8,128)(2,1)S(1)}, bf16[112,2048]{1,0:T(8,128)(2,1)S(1)}, bf16[112,2048]{1,0:T(8,128)(2,1)S(1)}) custom-call(s32[5]{0:T(128)S(1)} %stack.51.info_ref, s32[7296]{0:T(1024)S(1)} %constant_dynamic-update-slice_fusion.17.lists_ref, bf16[2,2,96,128,128]{4,3,2,1,0:T(8,128)(2,1)S(1)} %bitcast.112, ...), custom_call_target="tpu_custom_call" | custom-call | flops 16000000000 | tf_op jit(solution)/shard_map/pallas_call | solution.py:270
  144.4 1.3 collective-permute-start.10
  145.7 1.5 collective-permute-start.8
  147.2 1.3 collective-permute-start.11
  148.5 18.6 %shard_map.93 = (bf16[64,448,128]{2,1,0:T(8,128)(2,1)S(1)}, bf16[64,448,128]{2,1,0:T(8,128)(2,1)}, bf16[17,448,128]{2,1,0:T(8,128)(2,1)}) custom-call(s32[5]{0:T(128)S(1)} %stack.51.info_ref, s32[7296]{0:T(1024)S(1)} %constant_dynamic-update-slice_fusion.17.lists_ref, bf16[2,224,2048]{2,1,0:T(8,128)(2,1)} %bitcast.115, ...), custom_call_target="tpu_custom_call" | custom-call | flops 16000000000 | tf_op jit(solution)/shard_map/pallas_call | solution.py:270
  167.2 10.4 %shard_map.96 = (bf16[8,96,16,128]{3,2,1,0:T(8,128)(2,1)}, bf16[17,448,128]{2,1,0:T(8,128)(2,1)}) custom-call(s32[5]{0:T(128)S(1)} %stack.51.info_ref, s32[7296]{0:T(1024)S(1)} %constant_dynamic-update-slice_fusion.17.lists_ref, bf16[64,448,128]{2,1,0:T(8,128)(2,1)S(1)} %get-tuple-element.37.rest_0_, bf16[112,2048]{1,0:T(8,128)(2,1)S(1)} %collective-permute-done.8.rest_1_, ...), custom_call_target="tpu_custom_call" | custom-call | flops 8000000000 | tf_op jit(solution)/shard_map/pallas_call | solution.py:270
  177.6 25.4 %shard_map.97 = bf16[8,96,16,128]{3,2,1,0:T(8,128)(2,1)} custom-call(s32[5]{0:T(128)S(1)} %stack.51.info_ref, s32[7296]{0:T(1024)S(1)} %constant_dynamic-update-slice_fusion.17.lists_ref, bf16[17,448,128]{2,1,0:T(8,128)(2,1)} %get-tuple-element.36.rest_0_, bf16[17,448,128]{2,1,0:T(8,128)(2,1)} %get-tuple-element.45.rest_1_, ...), custom_call_target="tpu_custom_call" | custom-call | flops 16000000000 | tf_op jit(solution)/shard_map/pallas_call | solution.py:270
  203.1 21.9 %reduce-scatter.5.cloned.1.call-done = bf16[1,96,16,128]{3,2,1,0:T(8,128)(2,1)} async-done(((bf16[8,96,16,128]{3,2,1,0:T(8,128)(2,1)}), bf16[1,96,16,128]{3,2,1,0:T(8,128)(2,1)}) %reduce-scatter.5.cloned.1.call-update) | async-done | bytes 393232 | tf_op jit(solution)/shard_map/reduce_scatter | solution.py:842
  225.0 3.5 %adam.2 = (f32[2,96,16,128]{3,2,1,0:T(8,128)}, f32[2,96,16,128]{3,2,1,0:T(8,128)}) custom-call(bf16[96,16,128]{2,1,0:T(8,128)(2,1)} %bitcast.128, f32[2,96,16,128]{3,2,1,0:T(8,128)} %bitcast.119, f32[2,96,16,128]{3,2,1,0:T(8,128)} %bitcast.121, f32[2,96,16,128]{3,2,1,0:T(8,128)} %bitcast.123), custom_call_target="tpu_custom_call" | custom-call | tf_op jit(solution)/shard_map/adam/pallas_call | solution.py:671
  228.4 38.5 %reduce-scatter.3.cloned.1.call-done = bf16[1,96,16,128]{3,2,1,0:T(8,128)(2,1)} async-done(((bf16[8,96,16,128]{3,2,1,0:T(8,128)(2,1)}), bf16[1,96,16,128]{3,2,1,0:T(8,128)(2,1)}) %reduce-scatter.3.cloned.1.call-update) | async-done | bytes 393232 | tf_op jit(solution)/shard_map/reduce_scatter | solution.py:842
  267.0 3.5 %adam.3 = (f32[2,96,16,128]{3,2,1,0:T(8,128)}, f32[2,96,16,128]{3,2,1,0:T(8,128)}) custom-call(bf16[96,16,128]{2,1,0:T(8,128)(2,1)} %bitcast.127, f32[2,96,16,128]{3,2,1,0:T(8,128)} %bitcast.120, f32[2,96,16,128]{3,2,1,0:T(8,128)} %bitcast.122, f32[2,96,16,128]{3,2,1,0:T(8,128)} %bitcast.124, ...), custom_call_target="tpu_custom_call", output_to_operand_aliasing={{0}: (4, {}), {1}: (5, {})} | custom-call | tf_op jit(solution)/shard_map/adam/pallas_call | solution.py:671
  (47 shorter events, 1.0 us)
Async XLA Ops:
  7.2 217.8 %reduce-scatter.5.cloned.1.call-start = ((), (), s32[]{:S(2)}) async-start(), calls=%async_computation.3 | async-start | bytes 3538944 | tf_op jit(solution)/shard_map/reduce_scatter | solution.py:842
  19.9 14.9 %collective-permute-start.2 = (bf16[112,2048]{1,0:T(8,128)(2,1)S(1)}, bf16[112,2048]{1,0:T(8,128)(2,1)S(1)}, u32[]{:S(2)}, u32[]{:S(2)}) collective-permute-start(bf16[112,2048]{1,0:T(8,128)(2,1)S(1)} %shard_map.88), channel_id=1, source_target_pairs={{0,16},{24,8},{1,17},{25,9},{2,18},{26,10},{3,19},{27,11},{4,20},{... | collective-permute-start | bytes 1376264 | tf_op jit(solution)/shard_map/ppermute | solution.py:707
  32.4 20.1 %collective-permute-start = (bf16[112,2048]{1,0:T(8,128)(2,1)S(1)}, bf16[112,2048]{1,0:T(8,128)(2,1)S(1)}, u32[]{:S(2)}, u32[]{:S(2)}) collective-permute-start(bf16[112,2048]{1,0:T(8,128)(2,1)S(1)} %shard_map.86), channel_id=1, source_target_pairs={{0,8},{24,16},{1,9},{25,17},{2,10},{26,18},{3,11},{27,19},{4,12},{... | collective-permute-start | bytes 1376264 | tf_op jit(solution)/shard_map/ppermute | solution.py:707
  34.8 4.6 %copy-start = (bf16[1,2,2,96,128,128]{5,4,3,2,1,0:T(8,128)(2,1)S(1)}, bf16[1,2,2,96,128,128]{5,4,3,2,1,0:T(8,128)(2,1)}, u32[]{:S(2)}) copy-start(bf16[1,2,2,96,128,128]{5,4,3,2,1,0:T(8,128)(2,1)} %param.9) | copy-start | bytes 37748740
  51.2 14.6 %collective-permute-start.3 = (bf16[112,2048]{1,0:T(8,128)(2,1)S(1)}, bf16[112,2048]{1,0:T(8,128)(2,1)S(1)}, u32[]{:S(2)}, u32[]{:S(2)}) collective-permute-start(bf16[112,2048]{1,0:T(8,128)(2,1)S(1)} %get-tuple-element.29), channel_id=1, source_target_pairs={{16,0},{8,24},{17,1},{9,25},{18,2},{10,26},{19,3},{11,27},{20,4},{... | collective-permute-start | bytes 1376264 | tf_op jit(solution)/shard_map/ppermute | solution.py:710
  64.5 21.3 %collective-permute-start.1 = (bf16[112,2048]{1,0:T(8,128)(2,1)S(1)}, bf16[112,2048]{1,0:T(8,128)(2,1)S(1)}, u32[]{:S(2)}, u32[]{:S(2)}) collective-permute-start(bf16[112,2048]{1,0:T(8,128)(2,1)S(1)} %get-tuple-element.27), channel_id=1, source_target_pairs={{8,0},{16,24},{9,1},{17,25},{10,2},{18,26},{11,3},{19,27},{12,4},{... | collective-permute-start | bytes 1376264 | tf_op jit(solution)/shard_map/ppermute | solution.py:710
  77.4 67.0 %collective-permute-start.5 = (bf16[112,2048]{1,0:T(8,128)(2,1)S(1)}, bf16[112,2048]{1,0:T(8,128)(2,1)S(1)}, u32[]{:S(2)}, u32[]{:S(2)}) collective-permute-start(bf16[112,2048]{1,0:T(8,128)(2,1)S(1)} %get-tuple-element.31), channel_id=1, source_target_pairs={{0,24},{8,16},{16,8},{1,25},{9,17},{17,9},{2,26},{10,18},{18,10},{... | collective-permute-start | bytes 1376264 | tf_op jit(solution)/shard_map/ppermute | solution.py:722
  80.7 31.2 %collective-permute-start.6 = (bf16[112,2048]{1,0:T(8,128)(2,1)S(1)}, bf16[112,2048]{1,0:T(8,128)(2,1)S(1)}, u32[]{:S(2)}, u32[]{:S(2)}) collective-permute-start(bf16[112,2048]{1,0:T(8,128)(2,1)S(1)} %get-tuple-element.32), channel_id=1, source_target_pairs={{0,16},{24,8},{1,17},{25,9},{2,18},{26,10},{3,19},{27,11},{4,20},{... | collective-permute-start | bytes 1376264 | tf_op jit(solution)/shard_map/ppermute | solution.py:707
  85.9 59.8 %collective-permute-start.4 = (bf16[112,2048]{1,0:T(8,128)(2,1)S(1)}, bf16[112,2048]{1,0:T(8,128)(2,1)S(1)}, u32[]{:S(2)}, u32[]{:S(2)}) collective-permute-start(bf16[112,2048]{1,0:T(8,128)(2,1)S(1)} %select_select_fusion), channel_id=1, source_target_pairs={{0,24},{8,16},{16,8},{1,25},{9,17},{17,9},{2,26},{10,18},{18,10},{... | collective-permute-start | bytes 1376264 | tf_op jit(solution)/shard_map/ppermute | solution.py:722
  100.9 28.7 %collective-permute-start.7 = (bf16[112,2048]{1,0:T(8,128)(2,1)S(1)}, bf16[112,2048]{1,0:T(8,128)(2,1)S(1)}, u32[]{:S(2)}, u32[]{:S(2)}) collective-permute-start(bf16[112,2048]{1,0:T(8,128)(2,1)S(1)} %get-tuple-element.38), channel_id=1, source_target_pairs={{0,8},{24,16},{1,9},{25,17},{2,10},{26,18},{3,11},{27,19},{4,12},{... | collective-permute-start | bytes 1376264 | tf_op jit(solution)/shard_map/ppermute | solution.py:707
  127.0 40.1 %collective-permute-start.12 = (bf16[112,2048]{1,0:T(8,128)(2,1)S(1)}, bf16[112,2048]{1,0:T(8,128)(2,1)S(1)}, u32[]{:S(2)}, u32[]{:S(2)}) collective-permute-start(bf16[112,2048]{1,0:T(8,128)(2,1)S(1)} %shard_map.92.rest_12_), channel_id=1, source_target_pairs={{8,0},{9,1},{10,2},{11,3},{12,4},{13,5},{14,6},{15,7}} | collective-permute-start | bytes 1376264 | tf_op jit(solution)/shard_map/ppermute | solution.py:797
  128.3 38.8 %collective-permute-start.9 = (bf16[112,2048]{1,0:T(8,128)(2,1)S(1)}, bf16[112,2048]{1,0:T(8,128)(2,1)S(1)}, u32[]{:S(2)}, u32[]{:S(2)}) collective-permute-start(bf16[112,2048]{1,0:T(8,128)(2,1)S(1)} %shard_map.92.rest_12_), channel_id=1, source_target_pairs={{16,0},{17,1},{18,2},{19,3},{20,4},{21,5},{22,6},{23,7}} | collective-permute-start | bytes 1376264 | tf_op jit(solution)/shard_map/ppermute | solution.py:798
  129.6 17.6 %collective-permute-start.13 = (bf16[112,2048]{1,0:T(8,128)(2,1)S(1)}, bf16[112,2048]{1,0:T(8,128)(2,1)S(1)}, u32[]{:S(2)}, u32[]{:S(2)}) collective-permute-start(bf16[112,2048]{1,0:T(8,128)(2,1)S(1)} %get-tuple-element.44), channel_id=1, source_target_pairs={{0,24},{8,16},{16,8},{1,25},{9,17},{17,9},{2,26},{10,18},{18,10},{... | collective-permute-start | bytes 1376264 | tf_op jit(solution)/shard_map/ppermute | solution.py:722
  144.4 22.8 %collective-permute-start.10 = (bf16[112,2048]{1,0:T(8,128)(2,1)S(1)}, bf16[112,2048]{1,0:T(8,128)(2,1)S(1)}, u32[]{:S(2)}, u32[]{:S(2)}) collective-permute-start(bf16[112,2048]{1,0:T(8,128)(2,1)S(1)} %get-tuple-element.41), channel_id=1, source_target_pairs={{16,0},{17,1},{18,2},{19,3},{20,4},{21,5},{22,6},{23,7}} | collective-permute-start | bytes 1376264 | tf_op jit(solution)/shard_map/ppermute | solution.py:798
  145.7 21.5 %collective-permute-start.8 = (bf16[112,2048]{1,0:T(8,128)(2,1)S(1)}, bf16[112,2048]{1,0:T(8,128)(2,1)S(1)}, u32[]{:S(2)}, u32[]{:S(2)}) collective-permute-start(bf16[112,2048]{1,0:T(8,128)(2,1)S(1)} %get-tuple-element.41), channel_id=1, source_target_pairs={{8,0},{9,1},{10,2},{11,3},{12,4},{13,5},{14,6},{15,7}} | collective-permute-start | bytes 1376264 | tf_op jit(solution)/shard_map/ppermute | solution.py:797
  147.2 19.9 %collective-permute-start.11 = (bf16[112,2048]{1,0:T(8,128)(2,1)S(1)}, bf16[112,2048]{1,0:T(8,128)(2,1)S(1)}, u32[]{:S(2)}, u32[]{:S(2)}) collective-permute-start(bf16[112,2048]{1,0:T(8,128)(2,1)S(1)} %get-tuple-element.43), channel_id=1, source_target_pairs={{0,24},{8,16},{16,8},{1,25},{9,17},{17,9},{2,26},{10,18},{18,10},{... | collective-permute-start | bytes 1376264 | tf_op jit(solution)/shard_map/ppermute | solution.py:722
  177.6 89.4 %reduce-scatter.3.cloned.1.call-start = ((), (), s32[]{:S(2)}) async-start(), calls=%async_computation.2 | async-start | bytes 3538944 | tf_op jit(solution)/shard_map/reduce_scatter | solution.py:842
Sparse Core Ops, SparseCore 0:
  177.7 47.2 reduce-scatter.4
  227.3 39.6 reduce-scatter.2

commit v3 on v2

--- a/solution.py
+++ b/solution.py
@@ -505,7 +505,7 @@
                 slopes[part, c] = slope.astype(jnp.bfloat16)
 
             wide_pass(
-                normed.at[:, span], blocks_here, own.lists, UP_WIDE, sums, finish, False, 8
+                normed.at[:, span], blocks_here, own.lists, UP_WIDE, sums, finish, False, 16
             )
             put(part).start()
 
@@ -658,8 +658,10 @@
 
 def adam_call(share, part, state, token_total, filled=()):
     shape = state[0].shape
-    span = pl.BlockSpec((None,) + shape[1:], lambda i: (part, 0, 0, 0))
-    whole = pl.BlockSpec(share.shape, lambda i: (0, 0, 0))
+    pieces = 1
+    piece = shape[1] // pieces
+    span = pl.BlockSpec((None, piece) + shape[2:], lambda i: (part, i, 0, 0))
+    whole = pl.BlockSpec((piece,) + shape[2:], lambda i: (i, 0, 0))
 
     def kernel(share_ref, master_ref, moment_ref, variance_ref, *rest):
         direction, master_next = rest[-2:]
@@ -670,7 +672,7 @@
 
     return pl.pallas_call(
         kernel,
-        grid=(1,),
+        grid=(pieces,),
         in_specs=[whole] + [span] * 3 + [pl.BlockSpec(memory_space=pl.ANY)] * len(filled),
         out_specs=[span, span],
         out_shape=[shape_of(shape, jnp.float32)] * 2,

time: 278 us -> 277 us (level)
  transfers between devices with their start and end apart: 16 -> 16, of which waited for: 4 -> 4; matrix products, arithmetic and copies ran while one was open for 0% -> 0% of each run, Pallas kernels for 47% -> 46%
where the time goes in v3:
time: 277 us; the launch traced here: 276 us
  Pallas kernels  149 us (54%)
  waiting for transfers between devices  71 us (26%)
  starting transfers between devices  31.4 us (11%)
  between operations  14.5 us (5%)
  local copies, waits for them, and re-layouts  6.83 us (2%)
  other arithmetic  3.08 us (1%)
    pallas_call x12, Pallas kernels, stage(): pl.pallas_call(body, in_specs=[smem_spec, smem_spec] + [vmem_spec] * (len...  142 us
    reduce_scatter x2, waiting for transfers between devices, reduce(): return lax.psum_scatter(grads, 'dp', scatter_dimension=0, tiled=True)[0]  60.4 us
    ppermute x4, starting transfers between devices, inward(): return lax.ppermute(x, 'section', lane(i, h))  13 us
    ppermute x4, waiting for transfers between devices, inward(): return lax.ppermute(x, 'section', lane(i, h))  10.6 us
    ppermute x4, starting transfers between devices, swap(): return lax.ppermute(sent, 'section', pairs)  10.3 us
    pallas_call x2, Pallas kernels, adam_call(): pl.pallas_call(kernel, grid=(pieces,), in_specs=[whole] + [span] * 3 + [p...  6.93 us
  transfers between devices with their start and end apart: 16, of which 4 were waited for; matrix products, arithmetic and copies ran while one was open for 0% of the time, Pallas kernels for 46%

profile of v3, /device:TPU:0, one launch (start us, length us, event | category | flops | bytes accessed | tf_op | source)
XLA Modules:
  0.0 275.9 jit_solution(11142772909609177920)
XLA Ops:
  7.2 0.7 slice.20
  7.9 0.7 copy.60
  8.7 0.4 convert_reduce_fusion.2
  9.1 0.2 convert_reduce_fusion.3
  9.2 0.1 copy.58
  9.3 0.1 copy.57
  9.5 0.1 copy.55
  9.6 0.5 convert_reduce_fusion
  10.3 0.1 constant_dynamic-update-slice_fusion.4
  10.4 0.1 constant_dynamic-update-slice_fusion.2
  10.7 1.2 select_reduce_fusion
  12.1 0.1 reshape.400
  12.2 0.1 copy.56
  12.3 0.1 reshape_squeeze.3
  12.5 0.1 stack.51.info_ref
  12.6 7.3 %shard_map.88 = bf16[112,2048]{1,0:T(8,128)(2,1)S(1)} custom-call(s32[5]{0:T(128)S(1)} %stack.51.info_ref, s32[7296]{0:T(1024)S(1)} %constant_dynamic-update-slice_fusion.17.lists_ref, bf16[2,224,2048]{2,1,0:T(8,128)(2,1)} %bitcast.113, bf16[2,2,96,128,128]{4,3,2,1,0:T(8,128)(2,1)} %bitcast.102), custom_call_target="tpu_custom_call" | custom-call | flops 4000000000 | tf_op jit(solution)/shard_map/pallas_call | solution.py:270
  19.9 5.2 %collective-permute-start.2 = (bf16[112,2048]{1,0:T(8,128)(2,1)S(1)}, bf16[112,2048]{1,0:T(8,128)(2,1)S(1)}, u32[]{:S(2)}, u32[]{:S(2)}) collective-permute-start(bf16[112,2048]{1,0:T(8,128)(2,1)S(1)} %shard_map.88), channel_id=1, source_target_pairs={{0,16},{24,8},{1,17},{25,9},{2,18},{26,10},{3,19},{27,11},{4,20},{... | collective-permute-start | bytes 1376264 | tf_op jit(solution)/shard_map/ppermute | solution.py:709
  25.1 7.3 %shard_map.86 = bf16[112,2048]{1,0:T(8,128)(2,1)S(1)} custom-call(s32[5]{0:T(128)S(1)} %stack.51.info_ref, s32[7296]{0:T(1024)S(1)} %constant_dynamic-update-slice_fusion.17.lists_ref, bf16[2,224,2048]{2,1,0:T(8,128)(2,1)} %bitcast.114, bf16[2,2,96,128,128]{4,3,2,1,0:T(8,128)(2,1)} %bitcast.103), custom_call_target="tpu_custom_call" | custom-call | flops 4000000000 | tf_op jit(solution)/shard_map/pallas_call | solution.py:270
  32.4 1.5 collective-permute-start
  33.9 0.9 collective-permute-done.2.rest_1_.rest_3_.rest_6_
  34.8 4.6 %copy-done = bf16[1,2,2,96,128,128]{5,4,3,2,1,0:T(8,128)(2,1)S(1)} copy-done((bf16[1,2,2,96,128,128]{5,4,3,2,1,0:T(8,128)(2,1)S(1)}, bf16[1,2,2,96,128,128]{5,4,3,2,1,0:T(8,128)(2,1)}, u32[]{:S(2)}) %copy-start) | copy-done | bytes 12582936
  39.4 11.8 %shard_map.89 = (bf16[112,2048]{1,0:T(8,128)(2,1)S(1)}, bf16[112,2048]{1,0:T(8,128)(2,1)S(1)}, bf16[2,64,112,128]{3,2,1,0:T(8,128)(2,1)}) custom-call(s32[5]{0:T(128)S(1)} %stack.51.info_ref, s32[7296]{0:T(1024)S(1)} %constant_dynamic-update-slice_fusion.17.lists_ref, bf16[2,2,96,128,128]{4,3,2,1,0:T(8,128)(2,1)S(1)} %bitcast.106, ...), custom_call_target="tpu_custom_call" | custom-call | flops 8000000000 | tf_op jit(solution)/shard_map/pallas_call | solution.py:270
  51.2 1.3 collective-permute-start.3
  52.5 12.0 %shard_map.87 = (bf16[112,2048]{1,0:T(8,128)(2,1)S(1)}, bf16[112,2048]{1,0:T(8,128)(2,1)S(1)}, bf16[2,64,112,128]{3,2,1,0:T(8,128)(2,1)}) custom-call(s32[5]{0:T(128)S(1)} %stack.51.info_ref, s32[7296]{0:T(1024)S(1)} %constant_dynamic-update-slice_fusion.17.lists_ref, bf16[2,2,96,128,128]{4,3,2,1,0:T(8,128)(2,1)S(1)} %bitcast.107, ...), custom_call_target="tpu_custom_call" | custom-call | flops 8000000000 | tf_op jit(solution)/shard_map/pallas_call | solution.py:270
  64.5 1.3 collective-permute-start.1
  65.8 11.6 %shard_map.90 = (bf16[112,2048]{1,0:T(8,128)(2,1)S(1)}, bf16[112,2048]{1,0:T(8,128)(2,1)S(1)}, bf16[112,2048]{1,0:T(8,128)(2,1)S(1)}) custom-call(s32[5]{0:T(128)S(1)} %stack.51.info_ref, s32[7296]{0:T(1024)S(1)} %constant_dynamic-update-slice_fusion.17.lists_ref, bf16[2,2,96,128,128]{4,3,2,1,0:T(8,128)(2,1)S(1)} %bitcast.108, ...), custom_call_target="tpu_custom_call" | custom-call | flops 12000000000 | tf_op jit(solution)/shard_map/pallas_call | solution.py:270
  77.4 3.4 %collective-permute-start.5 = (bf16[112,2048]{1,0:T(8,128)(2,1)S(1)}, bf16[112,2048]{1,0:T(8,128)(2,1)S(1)}, u32[]{:S(2)}, u32[]{:S(2)}) collective-permute-start(bf16[112,2048]{1,0:T(8,128)(2,1)S(1)} %get-tuple-element.31), channel_id=1, source_target_pairs={{0,24},{8,16},{16,8},{1,25},{9,17},{17,9},{2,26},{10,18},{18,10},{... | collective-permute-start | bytes 1376264 | tf_op jit(solution)/shard_map/ppermute | solution.py:724
  80.7 5.1 %collective-permute-start.6 = (bf16[112,2048]{1,0:T(8,128)(2,1)S(1)}, bf16[112,2048]{1,0:T(8,128)(2,1)S(1)}, u32[]{:S(2)}, u32[]{:S(2)}) collective-permute-start(bf16[112,2048]{1,0:T(8,128)(2,1)S(1)} %get-tuple-element.32), channel_id=1, source_target_pairs={{0,16},{24,8},{1,17},{25,9},{2,18},{26,10},{3,19},{27,11},{4,20},{... | collective-permute-start | bytes 1376264 | tf_op jit(solution)/shard_map/ppermute | solution.py:709
  85.9 3.4 %collective-permute-start.4 = (bf16[112,2048]{1,0:T(8,128)(2,1)S(1)}, bf16[112,2048]{1,0:T(8,128)(2,1)S(1)}, u32[]{:S(2)}, u32[]{:S(2)}) collective-permute-start(bf16[112,2048]{1,0:T(8,128)(2,1)S(1)} %select_select_fusion), channel_id=1, source_target_pairs={{0,24},{8,16},{16,8},{1,25},{9,17},{17,9},{2,26},{10,18},{18,10},{... | collective-permute-start | bytes 1376264 | tf_op jit(solution)/shard_map/ppermute | solution.py:724
  89.3 11.6 %shard_map.94 = (bf16[112,2048]{1,0:T(8,128)(2,1)S(1)}, bf16[112,2048]{1,0:T(8,128)(2,1)S(1)}) custom-call(s32[5]{0:T(128)S(1)} %stack.51.info_ref, s32[7296]{0:T(1024)S(1)} %constant_dynamic-update-slice_fusion.17.lists_ref, bf16[2,2,96,128,128]{4,3,2,1,0:T(8,128)(2,1)S(1)} %bitcast.109, bf16[112,2048]{1,0:T(8,128)(2,1)S(1)} %collective-permute-done.1.rest_1_, ...), custom_call_target="tpu_custom_call" | custom-call | flops 12000000000 | tf_op jit(solution)/shard_map/pallas_call | solution.py:270
  100.9 1.3 collective-permute-start.7
  102.2 9.7 %collective-permute-done.6.rest_2_.rest_8_ = bf16[112,2048]{1,0:T(8,128)(2,1)S(1)} collective-permute-done((bf16[112,2048]{1,0:T(8,128)(2,1)S(1)}, bf16[112,2048]{1,0:T(8,128)(2,1)S(1)}, u32[]{:S(2)}, u32[]{:S(2)}) %collective-permute-start.6) | collective-permute-done | bytes 458784 | tf_op jit(solution)/shard_map/ppermute | solution.py:709
  111.9 7.5 %shard_map.91 = (bf16[112,2048]{1,0:T(8,128)(2,1)S(1)}, bf16[112,2048]{1,0:T(8,128)(2,1)S(1)}) custom-call(s32[5]{0:T(128)S(1)} %stack.51.info_ref, s32[7296]{0:T(1024)S(1)} %constant_dynamic-update-slice_fusion.17.lists_ref, bf16[2,2,96,128,128]{4,3,2,1,0:T(8,128)(2,1)S(1)} %bitcast.110, bf16[112,2048]{1,0:T(8,128)(2,1)S(1)} %get-tuple-element.30.rest_2_.rest_1_.rest_7_, ...), custom_call_target="tpu_custom_call" | custom-call | flops 8000000000 | tf_op jit(solution)/shard_map/pallas_call | solution.py:270
  119.5 7.5 %shard_map.92.rest_12_ = bf16[112,2048]{1,0:T(8,128)(2,1)S(1)} custom-call(s32[5]{0:T(128)S(1)} %stack.51.info_ref, s32[7296]{0:T(1024)S(1)} %constant_dynamic-update-slice_fusion.17.lists_ref, bf16[2,2,96,128,128]{4,3,2,1,0:T(8,128)(2,1)S(1)} %bitcast.111, bf16[112,2048]{1,0:T(8,128)(2,1)S(1)} %collective-permute-done.2.rest_1_.rest_3_.rest_6_, ...), custom_call_target="tpu_custom_call" | custom-call | flops 8000000000 | tf_op jit(solution)/shard_map/pallas_call | solution.py:270
  127.0 1.3 collective-permute-start.12
  128.3 1.3 collective-permute-start.9
  129.6 2.2 collective-permute-start.13
  131.8 12.6 %shard_map.95 = (bf16[112,2048]{1,0:T(8,128)(2,1)S(1)}, bf16[112,2048]{1,0:T(8,128)(2,1)S(1)}, bf16[112,2048]{1,0:T(8,128)(2,1)S(1)}) custom-call(s32[5]{0:T(128)S(1)} %stack.51.info_ref, s32[7296]{0:T(1024)S(1)} %constant_dynamic-update-slice_fusion.17.lists_ref, bf16[2,2,96,128,128]{4,3,2,1,0:T(8,128)(2,1)S(1)} %bitcast.112, ...), custom_call_target="tpu_custom_call" | custom-call | flops 16000000000 | tf_op jit(solution)/shard_map/pallas_call | solution.py:270
  144.4 1.3 collective-permute-start.10
  145.7 1.5 collective-permute-start.8
  147.2 1.3 collective-permute-start.11
  148.5 17.3 %shard_map.93 = (bf16[64,448,128]{2,1,0:T(8,128)(2,1)S(1)}, bf16[64,448,128]{2,1,0:T(8,128)(2,1)}, bf16[17,448,128]{2,1,0:T(8,128)(2,1)}) custom-call(s32[5]{0:T(128)S(1)} %stack.51.info_ref, s32[7296]{0:T(1024)S(1)} %constant_dynamic-update-slice_fusion.17.lists_ref, bf16[2,224,2048]{2,1,0:T(8,128)(2,1)} %bitcast.115, ...), custom_call_target="tpu_custom_call" | custom-call | flops 16000000000 | tf_op jit(solution)/shard_map/pallas_call | solution.py:270
  165.9 10.4 %shard_map.96 = (bf16[8,96,16,128]{3,2,1,0:T(8,128)(2,1)}, bf16[17,448,128]{2,1,0:T(8,128)(2,1)}) custom-call(s32[5]{0:T(128)S(1)} %stack.51.info_ref, s32[7296]{0:T(1024)S(1)} %constant_dynamic-update-slice_fusion.17.lists_ref, bf16[64,448,128]{2,1,0:T(8,128)(2,1)S(1)} %get-tuple-element.37.rest_0_, bf16[112,2048]{1,0:T(8,128)(2,1)S(1)} %collective-permute-done.8.rest_1_, ...), custom_call_target="tpu_custom_call" | custom-call | flops 8000000000 | tf_op jit(solution)/shard_map/pallas_call | solution.py:270
  176.4 25.4 %shard_map.97 = bf16[8,96,16,128]{3,2,1,0:T(8,128)(2,1)} custom-call(s32[5]{0:T(128)S(1)} %stack.51.info_ref, s32[7296]{0:T(1024)S(1)} %constant_dynamic-update-slice_fusion.17.lists_ref, bf16[17,448,128]{2,1,0:T(8,128)(2,1)} %get-tuple-element.36.rest_0_, bf16[17,448,128]{2,1,0:T(8,128)(2,1)} %get-tuple-element.45.rest_1_, ...), custom_call_target="tpu_custom_call" | custom-call | flops 16000000000 | tf_op jit(solution)/shard_map/pallas_call | solution.py:270
  201.8 21.9 %reduce-scatter.5.cloned.1.call-done = bf16[1,96,16,128]{3,2,1,0:T(8,128)(2,1)} async-done(((bf16[8,96,16,128]{3,2,1,0:T(8,128)(2,1)}), bf16[1,96,16,128]{3,2,1,0:T(8,128)(2,1)}) %reduce-scatter.5.cloned.1.call-update) | async-done | bytes 393232 | tf_op jit(solution)/shard_map/reduce_scatter | solution.py:844
  223.7 3.5 %adam.2 = (f32[2,96,16,128]{3,2,1,0:T(8,128)}, f32[2,96,16,128]{3,2,1,0:T(8,128)}) custom-call(bf16[96,16,128]{2,1,0:T(8,128)(2,1)} %bitcast.128, f32[2,96,16,128]{3,2,1,0:T(8,128)} %bitcast.119, f32[2,96,16,128]{3,2,1,0:T(8,128)} %bitcast.121, f32[2,96,16,128]{3,2,1,0:T(8,128)} %bitcast.123), custom_call_target="tpu_custom_call" | custom-call | tf_op jit(solution)/shard_map/adam/pallas_call | solution.py:673
  227.2 38.4 %reduce-scatter.3.cloned.1.call-done = bf16[1,96,16,128]{3,2,1,0:T(8,128)(2,1)} async-done(((bf16[8,96,16,128]{3,2,1,0:T(8,128)(2,1)}), bf16[1,96,16,128]{3,2,1,0:T(8,128)(2,1)}) %reduce-scatter.3.cloned.1.call-update) | async-done | bytes 393232 | tf_op jit(solution)/shard_map/reduce_scatter | solution.py:844
  265.6 3.5 %adam.3 = (f32[2,96,16,128]{3,2,1,0:T(8,128)}, f32[2,96,16,128]{3,2,1,0:T(8,128)}) custom-call(bf16[96,16,128]{2,1,0:T(8,128)(2,1)} %bitcast.127, f32[2,96,16,128]{3,2,1,0:T(8,128)} %bitcast.120, f32[2,96,16,128]{3,2,1,0:T(8,128)} %bitcast.122, f32[2,96,16,128]{3,2,1,0:T(8,128)} %bitcast.124, ...), custom_call_target="tpu_custom_call", output_to_operand_aliasing={{0}: (4, {}), {1}: (5, {})} | custom-call | tf_op jit(solution)/shard_map/adam/pallas_call | solution.py:673
  (47 shorter events, 1.0 us)
Async XLA Ops:
  7.2 216.5 %reduce-scatter.5.cloned.1.call-start = ((), (), s32[]{:S(2)}) async-start(), calls=%async_computation.3 | async-start | bytes 3538944 | tf_op jit(solution)/shard_map/reduce_scatter | solution.py:844
  19.9 14.9 %collective-permute-start.2 = (bf16[112,2048]{1,0:T(8,128)(2,1)S(1)}, bf16[112,2048]{1,0:T(8,128)(2,1)S(1)}, u32[]{:S(2)}, u32[]{:S(2)}) collective-permute-start(bf16[112,2048]{1,0:T(8,128)(2,1)S(1)} %shard_map.88), channel_id=1, source_target_pairs={{0,16},{24,8},{1,17},{25,9},{2,18},{26,10},{3,19},{27,11},{4,20},{... | collective-permute-start | bytes 1376264 | tf_op jit(solution)/shard_map/ppermute | solution.py:709
  32.4 20.1 %collective-permute-start = (bf16[112,2048]{1,0:T(8,128)(2,1)S(1)}, bf16[112,2048]{1,0:T(8,128)(2,1)S(1)}, u32[]{:S(2)}, u32[]{:S(2)}) collective-permute-start(bf16[112,2048]{1,0:T(8,128)(2,1)S(1)} %shard_map.86), channel_id=1, source_target_pairs={{0,8},{24,16},{1,9},{25,17},{2,10},{26,18},{3,11},{27,19},{4,12},{... | collective-permute-start | bytes 1376264 | tf_op jit(solution)/shard_map/ppermute | solution.py:709
  34.8 4.6 %copy-start = (bf16[1,2,2,96,128,128]{5,4,3,2,1,0:T(8,128)(2,1)S(1)}, bf16[1,2,2,96,128,128]{5,4,3,2,1,0:T(8,128)(2,1)}, u32[]{:S(2)}) copy-start(bf16[1,2,2,96,128,128]{5,4,3,2,1,0:T(8,128)(2,1)} %param.9) | copy-start | bytes 37748740
  51.2 14.6 %collective-permute-start.3 = (bf16[112,2048]{1,0:T(8,128)(2,1)S(1)}, bf16[112,2048]{1,0:T(8,128)(2,1)S(1)}, u32[]{:S(2)}, u32[]{:S(2)}) collective-permute-start(bf16[112,2048]{1,0:T(8,128)(2,1)S(1)} %get-tuple-element.29), channel_id=1, source_target_pairs={{16,0},{8,24},{17,1},{9,25},{18,2},{10,26},{19,3},{11,27},{20,4},{... | collective-permute-start | bytes 1376264 | tf_op jit(solution)/shard_map/ppermute | solution.py:712
  64.5 21.3 %collective-permute-start.1 = (bf16[112,2048]{1,0:T(8,128)(2,1)S(1)}, bf16[112,2048]{1,0:T(8,128)(2,1)S(1)}, u32[]{:S(2)}, u32[]{:S(2)}) collective-permute-start(bf16[112,2048]{1,0:T(8,128)(2,1)S(1)} %get-tuple-element.27), channel_id=1, source_target_pairs={{8,0},{16,24},{9,1},{17,25},{10,2},{18,26},{11,3},{19,27},{12,4},{... | collective-permute-start | bytes 1376264 | tf_op jit(solution)/shard_map/ppermute | solution.py:712
  77.4 67.0 %collective-permute-start.5 = (bf16[112,2048]{1,0:T(8,128)(2,1)S(1)}, bf16[112,2048]{1,0:T(8,128)(2,1)S(1)}, u32[]{:S(2)}, u32[]{:S(2)}) collective-permute-start(bf16[112,2048]{1,0:T(8,128)(2,1)S(1)} %get-tuple-element.31), channel_id=1, source_target_pairs={{0,24},{8,16},{16,8},{1,25},{9,17},{17,9},{2,26},{10,18},{18,10},{... | collective-permute-start | bytes 1376264 | tf_op jit(solution)/shard_map/ppermute | solution.py:724
  80.7 31.2 %collective-permute-start.6 = (bf16[112,2048]{1,0:T(8,128)(2,1)S(1)}, bf16[112,2048]{1,0:T(8,128)(2,1)S(1)}, u32[]{:S(2)}, u32[]{:S(2)}) collective-permute-start(bf16[112,2048]{1,0:T(8,128)(2,1)S(1)} %get-tuple-element.32), channel_id=1, source_target_pairs={{0,16},{24,8},{1,17},{25,9},{2,18},{26,10},{3,19},{27,11},{4,20},{... | collective-permute-start | bytes 1376264 | tf_op jit(solution)/shard_map/ppermute | solution.py:709
  85.9 59.8 %collective-permute-start.4 = (bf16[112,2048]{1,0:T(8,128)(2,1)S(1)}, bf16[112,2048]{1,0:T(8,128)(2,1)S(1)}, u32[]{:S(2)}, u32[]{:S(2)}) collective-permute-start(bf16[112,2048]{1,0:T(8,128)(2,1)S(1)} %select_select_fusion), channel_id=1, source_target_pairs={{0,24},{8,16},{16,8},{1,25},{9,17},{17,9},{2,26},{10,18},{18,10},{... | collective-permute-start | bytes 1376264 | tf_op jit(solution)/shard_map/ppermute | solution.py:724
  100.9 28.7 %collective-permute-start.7 = (bf16[112,2048]{1,0:T(8,128)(2,1)S(1)}, bf16[112,2048]{1,0:T(8,128)(2,1)S(1)}, u32[]{:S(2)}, u32[]{:S(2)}) collective-permute-start(bf16[112,2048]{1,0:T(8,128)(2,1)S(1)} %get-tuple-element.38), channel_id=1, source_target_pairs={{0,8},{24,16},{1,9},{25,17},{2,10},{26,18},{3,11},{27,19},{4,12},{... | collective-permute-start | bytes 1376264 | tf_op jit(solution)/shard_map/ppermute | solution.py:709
  127.0 38.9 %collective-permute-start.12 = (bf16[112,2048]{1,0:T(8,128)(2,1)S(1)}, bf16[112,2048]{1,0:T(8,128)(2,1)S(1)}, u32[]{:S(2)}, u32[]{:S(2)}) collective-permute-start(bf16[112,2048]{1,0:T(8,128)(2,1)S(1)} %shard_map.92.rest_12_), channel_id=1, source_target_pairs={{8,0},{9,1},{10,2},{11,3},{12,4},{13,5},{14,6},{15,7}} | collective-permute-start | bytes 1376264 | tf_op jit(solution)/shard_map/ppermute | solution.py:799
  128.3 37.6 %collective-permute-start.9 = (bf16[112,2048]{1,0:T(8,128)(2,1)S(1)}, bf16[112,2048]{1,0:T(8,128)(2,1)S(1)}, u32[]{:S(2)}, u32[]{:S(2)}) collective-permute-start(bf16[112,2048]{1,0:T(8,128)(2,1)S(1)} %shard_map.92.rest_12_), channel_id=1, source_target_pairs={{16,0},{17,1},{18,2},{19,3},{20,4},{21,5},{22,6},{23,7}} | collective-permute-start | bytes 1376264 | tf_op jit(solution)/shard_map/ppermute | solution.py:800
  129.6 17.6 %collective-permute-start.13 = (bf16[112,2048]{1,0:T(8,128)(2,1)S(1)}, bf16[112,2048]{1,0:T(8,128)(2,1)S(1)}, u32[]{:S(2)}, u32[]{:S(2)}) collective-permute-start(bf16[112,2048]{1,0:T(8,128)(2,1)S(1)} %get-tuple-element.44), channel_id=1, source_target_pairs={{0,24},{8,16},{16,8},{1,25},{9,17},{17,9},{2,26},{10,18},{18,10},{... | collective-permute-start | bytes 1376264 | tf_op jit(solution)/shard_map/ppermute | solution.py:724
  144.4 21.5 %collective-permute-start.10 = (bf16[112,2048]{1,0:T(8,128)(2,1)S(1)}, bf16[112,2048]{1,0:T(8,128)(2,1)S(1)}, u32[]{:S(2)}, u32[]{:S(2)}) collective-permute-start(bf16[112,2048]{1,0:T(8,128)(2,1)S(1)} %get-tuple-element.41), channel_id=1, source_target_pairs={{16,0},{17,1},{18,2},{19,3},{20,4},{21,5},{22,6},{23,7}} | collective-permute-start | bytes 1376264 | tf_op jit(solution)/shard_map/ppermute | solution.py:800
  145.7 20.2 %collective-permute-start.8 = (bf16[112,2048]{1,0:T(8,128)(2,1)S(1)}, bf16[112,2048]{1,0:T(8,128)(2,1)S(1)}, u32[]{:S(2)}, u32[]{:S(2)}) collective-permute-start(bf16[112,2048]{1,0:T(8,128)(2,1)S(1)} %get-tuple-element.41), channel_id=1, source_target_pairs={{8,0},{9,1},{10,2},{11,3},{12,4},{13,5},{14,6},{15,7}} | collective-permute-start | bytes 1376264 | tf_op jit(solution)/shard_map/ppermute | solution.py:799
  147.2 18.6 %collective-permute-start.11 = (bf16[112,2048]{1,0:T(8,128)(2,1)S(1)}, bf16[112,2048]{1,0:T(8,128)(2,1)S(1)}, u32[]{:S(2)}, u32[]{:S(2)}) collective-permute-start(bf16[112,2048]{1,0:T(8,128)(2,1)S(1)} %get-tuple-element.43), channel_id=1, source_target_pairs={{0,24},{8,16},{16,8},{1,25},{9,17},{17,9},{2,26},{10,18},{18,10},{... | collective-permute-start | bytes 1376264 | tf_op jit(solution)/shard_map/ppermute | solution.py:724
  176.3 89.3 %reduce-scatter.3.cloned.1.call-start = ((), (), s32[]{:S(2)}) async-start(), calls=%async_computation.2 | async-start | bytes 3538944 | tf_op jit(solution)/shard_map/reduce_scatter | solution.py:844
Sparse Core Ops, SparseCore 0:
  176.4 47.2 reduce-scatter.4
  226.0 39.5 reduce-scatter.2
